TPU v7x, 32 devices: a whole 2x2x4 slice. The times are simulated.
32 devices in a mesh: groups: 2 (over y), vis: 8 (over z, x), band: 2 (over core).
Axes of the slice: x: 2, y: 2, z: 4, core: 2. Of those that a mesh axis runs over, the one named last changes fastest.
Arguments:
- pieces: bfloat16 [2, 3072, 128, 128], P('band', ('groups', 'vis')), parts along dimension 1, may hold values from -6 to 6
- visit: int32 [2, 3072], P('band', ('groups', 'vis')), parts along dimension 1, may hold values from 0 to 23
- tile_map: int32 [2, 3072, 1], P('band', ('groups', 'vis')), parts along dimension 1, may hold values from 0 to 7; in each aligned block of 192 rows (0 to 191, 192 to 383, ..., all dimensions but the last counted through in order) at most 48 rows name the same one
- good_columns: int32 [2, 3072, 4], P('band', ('groups', 'vis')), parts along dimension 1, may hold values from -2147483648 to 2147483646, as said below
- psf_taps: float32 [2, 3072, 2, 21], P('band', ('groups', 'vis')), parts along dimension 1, may hold values from 0.05 to 1
- shifts: float32 [2, 3072, 2], P('band', ('groups', 'vis')), parts along dimension 1, may hold values from -0.5 to 0.5
- calib: float32 [2, 24], P('band'), may hold values from 0.5 to 2
- weights: int32 [2, 24], P('band'), may hold values from 1 to 8
- band_gain: float32 [2], P('band'), may hold values from 0.5 to 2
Outputs:
- coadd: float32 [2, 2048, 128], P('band', ('groups', 'vis')), parts along dimension 1
- detection: float32 [2048, 128], P(('groups', 'vis')), parts along dimension 0
There are 2 independent parts, one for each index of `groups`. A program takes and returns all parts, laid end to end along the dimension named above; an argument that names none is the same for every part. Nothing has to cross between parts.
Inputs may be any that keep to these rules, and one draw needn't show every extreme that they name: `tile_map`: among the 192 pieces of one band on one index of vis (aligned blocks of 192 pieces), no tile appears more than 48 times, a bound that some block reaches. `good_columns`: independent random bits.
All inputs are finite; a program needn't handle non-finite values.
Results may differ from a plain program's by a relative error of at most 0.0081.
Values may be sent and summed in bfloat16 or wider, within the bound.
No kernel may reach another device: no remote copies, remote signals or barrier semaphores. Data moves between devices by JAX's collectives and lax.ppermute only.
A program may use at most 128 MiB of HBM per device.

v0:
```python
import jax
import jax.numpy as jnp
from jax import lax
from jax.sharding import PartitionSpec as P


def good_mask(words):
    bits = jnp.arange(32, dtype=jnp.int32)
    flags = jnp.right_shift(words[..., None], bits) & 1
    return flags.reshape(words.shape[:-1] + (words.shape[-1] * 32,)).astype(jnp.float32)


def kernel_matrix(taps, size):
    kernel = taps / jnp.sum(taps, axis=-1, keepdims=True)
    count = taps.shape[-1]
    reach = (count - 1) // 2
    places = jnp.arange(size, dtype=jnp.int32)
    offset = places[None, :] - places[:, None] + reach
    table = (offset[None, :, :] == jnp.arange(count, dtype=jnp.int32)[:, None, None]).astype(
        jnp.float32
    )
    result = jnp.einsum("pt,tij->pij", kernel, table, precision=lax.Precision.HIGHEST)
    return result.astype(jnp.bfloat16)


def lanczos(values):
    inside = jnp.abs(values) < 3.0
    return jnp.where(inside, jnp.sinc(values) * jnp.sinc(values / 3.0), 0.0)


def warp_matrix(offset, size):
    places = jnp.arange(size).astype(jnp.float32)
    spread = places[None, None, :] - places[None, :, None] - offset[:, None, None]
    steps = jnp.arange(-3, 4).astype(jnp.float32)
    norms = jnp.sum(lanczos(steps[None, :] - offset[:, None]), axis=1)
    return (lanczos(spread) / norms[:, None, None]).astype(jnp.bfloat16)


def warp_pieces(pieces, visit, words, taps, shifts, calib, weights):
    size = pieces.shape[-1]
    good = good_mask(words)
    match = (visit[:, None] == jnp.arange(calib.shape[0], dtype=jnp.int32)[None, :]).astype(
        jnp.float32
    )
    scale = jnp.dot(match, calib, precision=lax.Precision.HIGHEST)
    weight = jnp.sum(match * weights.astype(jnp.float32)[None, :], axis=1)
    calibrated = (pieces.astype(jnp.float32) * scale[:, None, None] * good[:, None, :]).astype(
        jnp.bfloat16
    )
    w_rows = warp_matrix(shifts[:, 0], size)
    w_cols = warp_matrix(shifts[:, 1], size)
    k_rows = kernel_matrix(taps[:, 0], size)
    k_cols = kernel_matrix(taps[:, 1], size)
    left = jnp.einsum("pij,pjk->pik", w_rows, k_rows, preferred_element_type=jnp.float32).astype(
        jnp.bfloat16
    )
    right = jnp.einsum("pij,pjk->pik", w_cols, k_cols, preferred_element_type=jnp.float32).astype(
        jnp.bfloat16
    )
    inner = jnp.einsum(
        "pij,pkj->pik", calibrated, right, preferred_element_type=jnp.float32
    ).astype(jnp.bfloat16)
    warped = jnp.einsum("pij,pjk->pik", left, inner, preferred_element_type=jnp.float32)
    num_piece = (warped * weight[:, None, None]).astype(jnp.bfloat16)
    row_weight = (jnp.sum(left.astype(jnp.float32), axis=2) * weight[:, None]).astype(jnp.bfloat16)
    col_good = jnp.einsum("pij,pj->pi", right.astype(jnp.float32), good).astype(jnp.bfloat16)
    return (num_piece, row_weight, col_good)


def shards(pieces, visit, tile_map, good_columns, psf_taps, shifts, calib, weights, band_gain):
    num_piece, row_weight, col_good = warp_pieces(
        pieces[0], visit[0], good_columns[0], psf_taps[0], shifts[0], calib[0], weights[0]
    )
    count = num_piece.shape[0]
    size = num_piece.shape[-1]
    owners = lax.axis_size("vis")
    capacity = max(2, 2 * count // owners)
    tile = tile_map[0, :, 0]
    onehot = (tile[:, None] == jnp.arange(owners, dtype=jnp.int32)[None, :]).astype(jnp.int32)
    before = jnp.cumsum(onehot, axis=0) - onehot
    rank = jnp.sum(before * onehot, axis=1)
    slot = tile * capacity + rank
    vectors = jnp.stack([row_weight, col_good], axis=1)
    vec_buffer = jnp.zeros((owners * capacity, 2, size), jnp.bfloat16).at[slot].set(vectors)
    got_vec = lax.all_to_all(vec_buffer, "vis", split_axis=0, concat_axis=0, tiled=True)
    flat = num_piece.reshape(count, size * size)
    select = (
        tile[:, None] == jnp.arange(1 * lax.axis_size("vis"), dtype=jnp.int32)[None, :]
    ).astype(jnp.bfloat16)
    summed = jnp.einsum("pc,pk->ck", select, flat, preferred_element_type=jnp.float32)
    total = lax.psum_scatter(
        summed.reshape(1 * lax.axis_size("vis"), size, size), "vis", scatter_dimension=0, tiled=True
    )[0]
    den = jnp.dot(got_vec[:, 0, :].T, got_vec[:, 1, :], preferred_element_type=jnp.float32)
    coadd = total / jnp.maximum(den, 1.0)
    detection = lax.psum(band_gain[0] * coadd, "band")
    return (coadd[None], detection)


def solution(mesh):
    placed = (
        P("band", ("groups", "vis"), None, None),
        P("band", ("groups", "vis")),
        P("band", ("groups", "vis"), None),
        P("band", ("groups", "vis"), None),
        P("band", ("groups", "vis"), None, None),
        P("band", ("groups", "vis"), None),
        P("band", None),
        P("band", None),
        P("band"),
    )
    return jax.shard_map(
        shards,
        mesh=mesh,
        in_specs=placed,
        out_specs=(P("band", ("groups", "vis"), None), P(("groups", "vis"), None)),
        check_vma=False,
    )
```

profile of v0, /device:TPU:0, one launch (start us, length us, event | category | flops | bytes accessed | tf_op | source)
XLA Modules:
  0.0 221.3 jit_solution(6516371349511531576)
XLA Ops:
  7.3 0.9 slice_reduce_fusion.2
  8.2 0.8 fusion.297
  9.0 0.7 convert_bitcast_fusion.2
  9.8 0.8 fusion.156
  10.6 0.7 copy.30
  11.3 1.3 select_reduce_fusion
  12.6 1.4 fusion.168
  14.0 5.3 %convolution_convert_fusion.1 = bf16[192,128,128]{2,0,1:T(8,128)(2,1)S(1)} fusion(s32[128,128]{1,0:T(8,128)S(1)} %subtract_add_fusion, f32[192,1,21]{0,1,2:T(1,128)S(1)} %get-tuple-element.10, f32[192]{0:T(256)S(1)} %get-tuple-element.4), kind=kOutput, calls=%fused_computation.173 | convolution fusion | flops 796217280 | bytes 6373888 | tf_op jit(solution)/shard_map/pt,tij->pij/dot_general | solution.py:22
  19.4 5.4 %convolution_convert_fusion = bf16[192,128,128]{2,0,1:T(8,128)(2,1)S(1)} fusion(s32[128,128]{1,0:T(8,128)S(1)} %subtract_add_fusion, f32[192,1,21]{0,1,2:T(1,128)S(1)} %get-tuple-element.11, f32[192]{0:T(256)S(1)} %get-tuple-element.5), kind=kOutput, calls=%fused_computation.172 | convolution fusion | flops 796217280 | bytes 6373888 | tf_op jit(solution)/shard_map/pt,tij->pij/dot_general | solution.py:22
  24.9 43.7 %convert_reduce_fusion = (f32[192,128]{1,0:T(8,128)S(1)}, bf16[192,128,128]{1,2,0:T(8,128)(2,1)}) fusion(bf16[192,128,128]{2,0,1:T(8,128)(2,1)S(1)} %convolution_convert_fusion.1, f32[192]{0:T(256)S(1)} %get-tuple-element.6, f32[192]{0:T(256)S(1)} %bitcast.116, f32[128,128]{1,0:T(8,128)S(1)} %broadcast_subtract_fusion), kind=kOutput, calls=%fused_computation.122 | convolution fusion | flops 1044357120 | bytes 12748288 | tf_op jit(solution)/shard_map/pij,pjk->pik/dot_general | solution.py:54
  68.6 40.1 %fusion.142 = bf16[192,128,128]{2,1,0:T(8,128)(2,1)} fusion(bf16[192,128,128]{2,0,1:T(8,128)(2,1)S(1)} %convolution_convert_fusion, f32[192]{0:T(256)S(1)} %get-tuple-element.7, f32[192]{0:T(256)S(1)} %bitcast.114, f32[128,128]{1,0:T(8,128)S(1)} %broadcast_subtract_fusion), kind=kOutput, calls=%fused_computation.174 | convolution fusion | flops 1038090240 | bytes 12649984 | tf_op jit(solution)/shard_map/pij,pjk->pik/dot_general | solution.py:57
  108.7 11.9 %multiply_convert_fusion = bf16[192,128,128]{2,1,0:T(8,128)(2,1)} fusion(f32[192]{0:T(256)S(1)} %copy-done.5, bf16[192,128,128]{1,2,0:T(8,128)(2,1)} %get-tuple-element.15, bf16[192,128,128]{2,1,0:T(8,128)(2,1)} %fusion.142, bf16[1,192,128,128]{3,2,1,0:T(8,128)(2,1)} %param.11, f32[192,128]{1,0:T(8,128)S(1)} %copy-done.3, f32[192]{0:T(256)S(1)} %bitcast.122), kind=kOutput, calls=%fused_computation.123 | convolution fusion | flops 1632632832 | bytes 25265664 | tf_op jit(solution)/shard_map/pij,pjk->pik/dot_general | solution.py:63
  120.6 6.2 %fusion.96 = f32[8,128,128]{2,0,1:T(8,128)S(1)} fusion(s32[192]{0:T(256)S(1)} %bitcast.107, bf16[24,8,128,128]{3,2,1,0:T(8,128)(2,1)} %bitcast.120), kind=kOutput, calls=%fused_computation.130 | convolution fusion | flops 50333184 | bytes 6816512 | tf_op jit(solution)/shard_map/pc,pk->ck/dot_general | solution.py:90
  126.8 0.9 copy.34
  128.0 6.1 %fusion.298 = f32[192,1,128]{2,1,0:T(1,128)S(1)} fusion(bf16[192,128,128]{2,1,0:T(8,128)(2,1)} %fusion.142, bf16[192,128,1]{1,2,0:T(2,128)(2,1)S(1)} %copy.37), kind=kOutput, calls=%fused_computation.373 | convolution fusion | flops 6291456 | bytes 6438912 | tf_op jit(solution)/shard_map/pij,pj->pi/dot_general | solution.py:66
  134.3 0.6 reduce-window.6
  135.2 0.8 broadcast_in_dim.22
  136.0 20.8 %scatter_fusion = bf16[384,2,128]{2,1,0:T(2,128)(2,1)} fusion(bf16[384,2,128]{2,1,0:T(2,128)(2,1)} %broadcast_in_dim.22, s32[192]{0:T(256)S(1)} %bitcast.110, bf16[192,2,128]{2,1,0:T(2,128)(2,1)S(1)} %copy.35), kind=kCustom, calls=%fused_computation | custom fusion | bytes 295680 | tf_op jit(solution)/shard_map/scatter | solution.py:84
  156.8 7.4 %all-to-all-start = ((bf16[384,2,128]{2,1,0:T(2,128)(2,1)}), bf16[384,2,128]{2,1,0:T(2,128)(2,1)S(1)}, u32[]{:S(2)}, u32[]{:S(2)}) async-start(bf16[384,2,128]{2,1,0:T(2,128)(2,1)} %scatter_fusion), calls=%async_computation.1 | async-start | bytes 393216 | tf_op jit(solution)/shard_map/all_to_all | solution.py:85
  165.0 7.2 %all-to-all-done = bf16[384,2,128]{2,1,0:T(2,128)(2,1)S(1)} async-done(((bf16[384,2,128]{2,1,0:T(2,128)(2,1)}), bf16[384,2,128]{2,1,0:T(2,128)(2,1)S(1)}, u32[]{:S(2)}, u32[]{:S(2)}) %all-to-all-start) | async-done | bytes 196640 | tf_op jit(solution)/shard_map/all_to_all | solution.py:85
  172.5 20.9 %reduce-scatter.2.cloned.1.call-done = f32[1,128,128]{2,1,0:T(8,128)} async-done(((f32[8,128,128]{2,1,0:T(8,128)}), f32[1,128,128]{2,1,0:T(8,128)}) %reduce-scatter.2.cloned.1.call-update) | async-done | bytes 65552 | tf_op jit(solution)/shard_map/reduce_scatter | solution.py:91
  193.3 1.7 broadcast_multiply_fusion
  195.1 17.9 %all-reduce.3.cloned.1.call-done = f32[128,128]{1,0:T(8,128)} async-done(((f32[128,128]{1,0:T(8,128)}), f32[128,128]{1,0:T(8,128)}) %all-reduce.3.cloned.1.call-update) | async-done | bytes 65552 | tf_op jit(solution)/shard_map/psum | solution.py:96
  212.9 1.5 copy.85
  (39 shorter events, 1.5 us)
Async XLA Ops:
  7.2 5.5 %copy-start = (f32[1,24]{1,0:T(1,128)S(1)}, f32[1,24]{1,0:T(1,128)}, u32[]{:S(2)}) copy-start(f32[1,24]{1,0:T(1,128)} %param.17) | copy-start | bytes 292
  7.2 186.2 %reduce-scatter.2.cloned.1.call-start = ((), (), s32[]{:S(2)}) async-start(), calls=%async_computation.2 | async-start | bytes 589824 | tf_op jit(solution)/shard_map/reduce_scatter | solution.py:91
  10.6 14.2 %copy-start.1 = (f32[192,128]{0,1:T(8,128)}, f32[192,128]{0,1:T(8,128)S(1)}, u32[]{:S(2)}) copy-start(f32[192,128]{0,1:T(8,128)S(1)} %fusion.156) | copy-start | bytes 294916
  68.6 40.1 %copy-start.3 = (f32[192,128]{1,0:T(8,128)S(1)}, f32[192,128]{1,0:T(8,128)}, u32[]{:S(2)}) copy-start(f32[192,128]{1,0:T(8,128)} %copy.30) | copy-start | bytes 294916
  68.6 40.1 %copy-start.5 = (f32[192]{0:T(256)S(1)}, f32[192]{0:T(256)}, u32[]{:S(2)}) copy-start(f32[192]{0:T(256)} %select_reduce_fusion) | copy-start | bytes 2308
  68.6 40.1 %copy-start.6 = (f32[1,192]{1,0:T(1,128)S(1)}, f32[1,192]{1,0:T(1,128)}, u32[]{:S(2)}) copy-start(f32[1,192]{1,0:T(1,128)} %fusion.168) | copy-start | bytes 2308
  108.7 11.9 %copy-start.4 = (s32[1,192,1]{1,2,0:T(1,128)S(1)}, s32[1,192,1]{1,2,0:T(1,128)}, u32[]{:S(2)}) copy-start(s32[1,192,1]{1,2,0:T(1,128)} %param.13) | copy-start | bytes 2308
  120.6 7.2 %copy-start.2 = (f32[192,128]{0,1:T(8,128)S(1)}, f32[192,128]{0,1:T(8,128)}, u32[]{:S(2)}) copy-start(f32[192,128]{0,1:T(8,128)} %copy-done.1) | copy-start | bytes 294916
  156.8 15.3 %all-to-all-start = ((bf16[384,2,128]{2,1,0:T(2,128)(2,1)}), bf16[384,2,128]{2,1,0:T(2,128)(2,1)S(1)}, u32[]{:S(2)}, u32[]{:S(2)}) async-start(bf16[384,2,128]{2,1,0:T(2,128)(2,1)} %scatter_fusion), calls=%async_computation.1 | async-start | bytes 393216 | tf_op jit(solution)/shard_map/all_to_all | solution.py:85
  164.3 48.7 %all-reduce.3.cloned.1.call-start = ((), (), s32[]{:S(2)}) async-start(), calls=%async_computation.3 | async-start | bytes 131072 | tf_op jit(solution)/shard_map/psum | solution.py:96
Sparse Core Ops, SparseCore 0:
  127.8 65.4 reduce-scatter.1
  196.2 16.7 all-reduce.2
where the time goes:
time: 222 us; the launch traced here: 221 us
  matrix products  122 us (55%)
  waiting for transfers between devices  46 us (21%)
  local copies, waits for them, and re-layouts  26.4 us (12%)
  between operations  14.9 us (7%)
  starting transfers between devices  7.49 us (3%)
  other arithmetic  4.79 us (2%)
    dot_general x1, matrix products, warp_pieces(): jnp.einsum('pij,pjk->pik', w_rows, k_rows, preferred_element_type=jnp.flo...  43.7 us
    dot_general x1, matrix products, warp_pieces(): jnp.einsum('pij,pjk->pik', w_cols, k_cols, preferred_element_type=jnp.flo...  40.1 us
    reduce_scatter x1, waiting for transfers between devices, shards(): lax.psum_scatter(summed.reshape(1 * lax.axis_size('vis'), size, size), 'v...  20.9 us
    scatter x1, local copies, waits for them, and re-layouts, shards(): jnp.zeros((owners * capacity, 2, size), jnp.bfloat16).at[slot].set(vectors)  20.8 us
    psum x1, waiting for transfers between devices, shards(): detection = lax.psum(band_gain[0] * coadd, 'band')  17.9 us
    dot_general x1, matrix products, warp_pieces(): jnp.einsum('pij,pjk->pik', left, inner, preferred_element_type=jnp.float32)  11.9 us
    dot_general x2, matrix products, kernel_matrix(): jnp.einsum('pt,tij->pij', kernel, table, precision=lax.Precision.HIGHEST)  10.7 us
    all_to_all x1, starting transfers between devices, shards(): lax.all_to_all(vec_buffer, 'vis', split_axis=0, concat_axis=0, tiled=True)  7.42 us
  transfers between devices with their start and end apart: 3, of which 3 were waited for; matrix products, arithmetic and copies ran while one was open for 13% of the time, Pallas kernels for 0%

commit v1 on v0

v1 whole, which is shorter than its diff:
```python
import functools

import jax
import jax.numpy as jnp
import numpy as np
from jax import lax
from jax.experimental import pallas as pl
from jax.experimental.pallas import tpu as pltpu
from jax.sharding import PartitionSpec as P

EDGE = 3
ROWS = 16
SLOT = 32
GROUP = 4


def sinc(values):
    zero = values == 0.0
    scaled = jnp.where(zero, 1.0, values) * np.float32(np.pi)
    return jnp.where(zero, 1.0, jnp.sin(scaled) / scaled)


def lanczos(values):
    inside = jnp.abs(values) < float(EDGE)
    return jnp.where(inside, sinc(values) * sinc(values / float(EDGE)), 0.0)


def tap_vectors(taps, shift, pad_ref):
    count, n = taps.shape
    kernel = (taps / jnp.sum(taps, axis=0, keepdims=True)).astype(jnp.bfloat16)
    steps = range(-EDGE, EDGE + 1)
    window = [lanczos(float(m) - shift) for m in steps]
    norm = functools.reduce(jnp.add, window)
    window = [(w / norm).astype(jnp.bfloat16).astype(jnp.float32) for w in window]
    pad_ref[...] = jnp.zeros_like(pad_ref)
    pad_ref[pl.ds(8, count), :] = kernel.astype(jnp.float32)
    terms = [window[m + EDGE] * pad_ref[pl.ds(8 - m - EDGE, SLOT), :] for m in steps]
    first = [functools.reduce(jnp.add, terms[EDGE:])]
    for m in range(EDGE - 1, -1, -1):
        first.append(first[-1] + terms[m])
    last = [functools.reduce(jnp.add, terms[: EDGE + 1])]
    for m in range(EDGE + 1, 2 * EDGE):
        last.append(last[-1] + terms[m])
    kinds = first + last[::-1]
    return jnp.concatenate(kinds, axis=0).astype(jnp.bfloat16)


def kind_of(place, size):
    low = jnp.minimum(place, EDGE)
    return jnp.where(place >= size - EDGE, place - (size - EDGE) + EDGE + 1, low)


def table_block(block, size, halo, side):
    if block == 0:
        low, high = 0, EDGE + 1
    elif block == 1:
        low, high = EDGE, EDGE + 1
    else:
        low, high = EDGE, 2 * EDGE + 1
    depth = (high - low) * SLOT
    start = {0: 0, 1: ROWS, 2: size - ROWS}[block]
    tap = lax.broadcasted_iota(jnp.int32, (depth, size), 0)
    lane = lax.broadcasted_iota(jnp.int32, (1, size), 1)
    chunks = []
    for r in range(ROWS):
        row = start + r
        if side == 0:
            d = lane - row + halo
            kind = min(row, EDGE) if row < size - EDGE else row - (size - EDGE) + EDGE + 1
            slot = (kind - low) * SLOT + d
        else:
            d = row - lane + halo
            slot = (kind_of(lane, size) - low) * SLOT + d
        slot = jnp.where((d >= 0) & (d <= 2 * halo), slot, -1)
        chunks.append((tap == slot).astype(jnp.float32).astype(jnp.bfloat16))
    return low * SLOT, high * SLOT, jnp.concatenate(chunks, axis=1)


def fill_base(vectors_t, base_ref, size, halo, side):
    n = vectors_t.shape[0]
    for block in range(3):
        low, high, table = table_block(block, size, halo, side)
        out = jnp.dot(vectors_t[:, low:high], table, preferred_element_type=jnp.float32)
        for r in range(ROWS):
            base_ref[pl.ds((block * ROWS + r) * n, n), :] = out[:, r * size : (r + 1) * size]


def build(base_ref, p, n, size):
    blocks = []
    for block in range(3):
        halves = [
            base_ref[pl.ds((block * ROWS + 8 * h) * n + p, 8, stride=n), :] for h in range(ROWS // 8)
        ]
        blocks.append(jnp.concatenate(halves, axis=0))
    inner = [
        pltpu.roll(blocks[1], ROWS * b, 1).astype(jnp.bfloat16) for b in range(size // ROWS - 2)
    ]
    return jnp.concatenate(
        [blocks[0].astype(jnp.bfloat16)] + inner + [blocks[2].astype(jnp.bfloat16)], axis=0
    )


def kernel(
    tiles,
    tile_s,
    visit_s,
    words_s,
    calib_s,
    weights_s,
    tile_v,
    visit_v,
    taps_v,
    shifts_v,
    pieces_h,
    out_v,
    pieces_v,
    left_base,
    right_base,
    pad_ref,
    acc,
    cover,
    sems,
):
    n, size, _ = pieces_h.shape
    count = taps_v.shape[0]
    halo = (count - 1) // 2 + EDGE
    chunks = sems.shape[0]
    share = n // chunks
    copies = [
        pltpu.make_async_copy(
            pieces_h.at[pl.ds(c * share, share)], pieces_v.at[pl.ds(c * share, share)], sems.at[c]
        )
        for c in range(chunks)
    ]
    for copy in copies:
        copy.start()
    acc[...] = jnp.zeros_like(acc)
    vectors = []
    for side, base_ref in ((0, left_base), (1, right_base)):
        vec = tap_vectors(taps_v[:, side, :], shifts_v[pl.ds(side, 1), :], pad_ref)
        vectors.append(vec)
        fill_base(vec.astype(jnp.float32).T.astype(jnp.bfloat16), base_ref, size, halo, side)
    lane = lax.broadcasted_iota(jnp.int32, (8, size), 1)
    bit = lane & 31
    for copy in copies:
        copy.wait()

    def step(g, carry):
        for k in range(GROUP):
            p = g * GROUP + k
            word = jnp.where(
                lane < 64,
                jnp.where(lane < 32, words_s[0, p], words_s[1, p]),
                jnp.where(lane < 96, words_s[2, p], words_s[3, p]),
            )
            mask = (jnp.right_shift(word, bit) & 1).astype(jnp.float32)
            mask = jnp.concatenate([mask, mask], axis=0).astype(jnp.bfloat16)
            piece = pieces_v[p]
            rows = [piece[16 * b : 16 * b + 16] * mask for b in range(size // 16)] + [mask]
            right = build(right_base, p, n, size)
            inner = jnp.dot(
                jnp.concatenate(rows, axis=0), right, preferred_element_type=jnp.float32
            )
            cover[pl.ds(p, 1), :] = inner[size : size + 1]
            v = visit_s[0, p]
            factor = calib_s[0, v] * weights_s[0, v].astype(jnp.float32)
            inner = (inner[:size] * factor).astype(jnp.bfloat16)
            left = build(left_base, p, n, size)
            acc[tile_s[0, p]] += jnp.dot(left, inner, preferred_element_type=jnp.float32)
        return carry

    lax.fori_loop(0, n // GROUP, step, 0)

    kinds = 2 * EDGE + 1
    place = lax.broadcasted_iota(jnp.int32, (SLOT, kinds * SLOT), 0)
    row = jnp.where(place <= halo, place, place - (2 * halo + 1) + size)
    column = lax.broadcasted_iota(jnp.int32, (SLOT, kinds * SLOT), 1)
    d = (column & (SLOT - 1)) + row - halo
    chosen = (column // SLOT == kind_of(row, size)) & (d >= 0) & (d < size) & (row < size)
    table = chosen.astype(jnp.float32).astype(jnp.bfloat16)
    weight = jnp.zeros((1, n), jnp.float32)
    for v in range(weights_s.shape[1]):
        weight = jnp.where(visit_v[...] == v, weights_s[0, v].astype(jnp.float32), weight)
    row_weight = jnp.dot(table, vectors[0], preferred_element_type=jnp.float32) * weight
    chosen_rows = [jnp.where(tile_v[...] == t, row_weight, 0.0) for t in range(tiles)]
    den = jnp.dot(
        jnp.concatenate(chosen_rows, axis=0).astype(jnp.bfloat16),
        cover[...].astype(jnp.bfloat16),
        preferred_element_type=jnp.float32,
    )
    for t in range(tiles):
        out_v[t, :size, :] = acc[t].astype(out_v.dtype)
        out_v[t, size:, :] = den[t * SLOT : (t + 1) * SLOT].astype(out_v.dtype)


def partial_sums(tiles, pieces, visit, tile, words, taps, shifts, calib, weights):
    n, size, _ = pieces.shape
    smem = pl.BlockSpec(memory_space=pltpu.SMEM)
    vmem = pl.BlockSpec(memory_space=pltpu.VMEM)
    return pl.pallas_call(
        functools.partial(kernel, tiles),
        out_shape=jax.ShapeDtypeStruct((tiles, size + SLOT, size), jnp.bfloat16),
        in_specs=[smem] * 5 + [vmem] * 4 + [pl.BlockSpec(memory_space=pl.ANY)],
        out_specs=vmem,
        scratch_shapes=[
            pltpu.VMEM((n, size, size), jnp.bfloat16),
            pltpu.VMEM((3 * ROWS * n, size), jnp.float32),
            pltpu.VMEM((3 * ROWS * n, size), jnp.float32),
            pltpu.VMEM((SLOT + 16, n), jnp.float32),
            pltpu.VMEM((tiles, size, size), jnp.float32),
            pltpu.VMEM((n, size), jnp.float32),
            pltpu.SemaphoreType.DMA((4,)),
        ],
        compiler_params=pltpu.CompilerParams(vmem_limit_bytes=56 * 1024 * 1024),
        name="partial_sums",
    )(tile, visit, words, calib, weights, tile, visit, taps, shifts, pieces)


def shards(pieces, visit, tile_map, good_columns, psf_taps, shifts, calib, weights, band_gain):
    size = pieces.shape[-1]
    tiles = lax.axis_size("vis")
    halo = (psf_taps.shape[-1] - 1) // 2 + EDGE
    sums = partial_sums(
        tiles,
        pieces[0],
        visit,
        tile_map[:, :, 0],
        good_columns[0].T,
        jnp.transpose(psf_taps[0], (2, 1, 0)),
        shifts[0].T,
        calib,
        weights,
    )
    got = lax.all_to_all(sums, "vis", split_axis=0, concat_axis=0, tiled=True)
    total = jnp.sum(got.astype(jnp.float32), axis=0)
    few = total[size:]
    den = jnp.concatenate(
        [
            few[:halo],
            jnp.broadcast_to(few[halo], (size - 2 * halo, size)),
            few[halo + 1 : 2 * halo + 1],
        ],
        axis=0,
    )
    coadd = total[:size] / jnp.maximum(den, 1.0)
    scaled = band_gain[0] * coadd
    detection = scaled
    bands = lax.axis_size("band")
    for k in range(1, bands):
        detection = detection + lax.ppermute(
            scaled, "band", [(b, (b + k) % bands) for b in range(bands)]
        )
    return (coadd[None], detection)


def solution(mesh):
    placed = (
        P("band", ("groups", "vis"), None, None),
        P("band", ("groups", "vis")),
        P("band", ("groups", "vis"), None),
        P("band", ("groups", "vis"), None),
        P("band", ("groups", "vis"), None, None),
        P("band", ("groups", "vis"), None),
        P("band", None),
        P("band", None),
        P("band"),
    )
    return jax.shard_map(
        shards,
        mesh=mesh,
        in_specs=placed,
        out_specs=(P("band", ("groups", "vis"), None), P(("groups", "vis"), None)),
        check_vma=False,
    )
```

time: 222 us -> 68.1 us (0.31)
  matrix products: 122 us -> 0 us
  Pallas kernels: 0 us -> 47 us
  waiting for transfers between devices: 46 us -> 10.9 us
  local copies, waits for them, and re-layouts: 26.4 us -> 0.02 us
  between operations: 14.9 us -> 1.32 us
  other arithmetic: 4.79 us -> 1.34 us
    dot_general x9 -> x0, matrix products: 122 us -> none  [the longest x1 43.7 us: warp_pieces(): jnp.einsum('pij,pjk->pik', w_rows, k_rows, preferred_element_type=jnp.flo...]
    pallas_call x0 -> x1, Pallas kernels: none -> 47 us  [partial_sums(): pl.pallas_call(functools.partial(kernel, tiles), out_shape=jax.ShapeDtype...]
    reduce_scatter x1 -> x0, waiting for transfers between devices: 20.9 us -> none  [shards(): lax.psum_scatter(summed.reshape(1 * lax.axis_size('vis'), size, size), 'v...]
    scatter x1 -> x0, local copies, waits for them, and re-layouts: 20.8 us -> none  [shards(): jnp.zeros((owners * capacity, 2, size), jnp.bfloat16).at[slot].set(vectors)]
    psum x1 -> x0, waiting for transfers between devices: 17.9 us -> none  [shards(): detection = lax.psum(band_gain[0] * coadd, 'band')]
    all_to_all x1, waiting for transfers between devices: 7.23 us -> 9.65 us  [shards(): got = lax.all_to_all(sums, 'vis', split_axis=0, concat_axis=0, tiled=True)]
    reduce_sum x4 -> x1, other arithmetic: 2.42 us -> 0.05 us  [shards(): total = jnp.sum(got.astype(jnp.float32), axis=0)]
  transfers between devices with their start and end apart: 3 -> 2, of which waited for: 3 -> 2; matrix products, arithmetic and copies ran while one was open for 13% -> 0% of each run, Pallas kernels for 0% -> 0%
where the time goes in v1:
time: 68.1 us; the launch traced here: 67.8 us
  Pallas kernels  47 us (69%)
  waiting for transfers between devices  10.9 us (16%)
  starting transfers between devices  7.29 us (11%)
  other arithmetic  1.34 us (2%)
  between operations  1.32 us (2%)
    pallas_call x1, Pallas kernels, partial_sums(): pl.pallas_call(functools.partial(kernel, tiles), out_shape=jax.ShapeDtype...  47 us
    all_to_all x1, waiting for transfers between devices, shards(): got = lax.all_to_all(sums, 'vis', split_axis=0, concat_axis=0, tiled=True)  9.65 us
    all_to_all x1, starting transfers between devices, shards(): got = lax.all_to_all(sums, 'vis', split_axis=0, concat_axis=0, tiled=True)  7.29 us
  transfers between devices with their start and end apart: 2, of which 2 were waited for; matrix products, arithmetic and copies ran while one was open for 0% of the time, Pallas kernels for 0%

profile of v1, /device:TPU:0, one launch (start us, length us, event | category | flops | bytes accessed | tf_op | source)
XLA Modules:
  0.0 67.8 jit_solution(1420160356715892504)
XLA Ops:
  0.6 47.0 %partial_sums.1 = bf16[8,160,128]{2,1,0:T(8,128)(2,1)} custom-call(s32[1,192]{1,0:T(1,128)} %bitcast.20, s32[1,192]{1,0:T(1,128)} %visit_v.1, s32[4,192]{1,0:T(4,128)} %bitcast.19, f32[1,24]{1,0:T(1,128)} %calib_s.1, s32[1,24]{1,0:T(1,128)} %weights_s.1, s32[1,192]{1,0:T(1,128)} %bitcast.21, s32[1,192]{1,0:T(1,128)} %visit_v.1, f32[21,2,192]{2,1,0:T(2,128)} %bitcast.18, ...), custom_call_target="tpu_custom_call" | custom-call | tf_op jit(solution)/shard_map/partial_sums/pallas_call | solution.py:200
  47.6 7.3 %all-to-all-start = ((bf16[8,160,128]{2,1,0:T(8,128)(2,1)}), bf16[8,160,128]{2,1,0:T(8,128)(2,1)S(1)}, u32[]{:S(2)}, u32[]{:S(2)}) async-start(bf16[8,160,128]{2,1,0:T(8,128)(2,1)} %partial_sums.1), calls=%async_computation | async-start | bytes 655360 | tf_op jit(solution)/shard_map/all_to_all | solution.py:234
  55.5 9.6 %all-to-all-done = bf16[8,160,128]{2,1,0:T(8,128)(2,1)S(1)} async-done(((bf16[8,160,128]{2,1,0:T(8,128)(2,1)}), bf16[8,160,128]{2,1,0:T(8,128)(2,1)S(1)}, u32[]{:S(2)}, u32[]{:S(2)}) %all-to-all-start) | async-done | bytes 327712 | tf_op jit(solution)/shard_map/all_to_all | solution.py:234
  65.3 0.7 broadcast_multiply_fusion
  65.9 0.0 collective-permute-start
  65.9 1.3 %collective-permute-done = f32[128,128]{1,0:T(8,128)S(1)} collective-permute-done((f32[128,128]{1,0:T(8,128)S(1)}, f32[128,128]{1,0:T(8,128)S(1)}, u32[]{:S(2)}, u32[]{:S(2)}) %collective-permute-start) | collective-permute-done | bytes 65568 | tf_op jit(solution)/shard_map/ppermute | solution.py:250
  67.2 0.6 add.3
  (4 shorter events, 0.1 us)
Async XLA Ops:
  47.6 17.6 %all-to-all-start = ((bf16[8,160,128]{2,1,0:T(8,128)(2,1)}), bf16[8,160,128]{2,1,0:T(8,128)(2,1)S(1)}, u32[]{:S(2)}, u32[]{:S(2)}) async-start(bf16[8,160,128]{2,1,0:T(8,128)(2,1)} %partial_sums.1), calls=%async_computation | async-start | bytes 655360 | tf_op jit(solution)/shard_map/all_to_all | solution.py:234
  65.9 1.3 %collective-permute-start = (f32[128,128]{1,0:T(8,128)S(1)}, f32[128,128]{1,0:T(8,128)S(1)}, u32[]{:S(2)}, u32[]{:S(2)}) collective-permute-start(f32[128,128]{1,0:T(8,128)S(1)} %get-tuple-element.2), channel_id=1, source_target_pairs={{0,1},{1,0},{2,3},{3,2},{4,5},{5,4},{6,7},{7,6},{8,9},{9,8},{10,11... | collective-permute-start | bytes 196616 | tf_op jit(solution)/shard_map/ppermute | solution.py:250

commit v2 on v1

--- a/solution.py
+++ b/solution.py
@@ -11,7 +11,8 @@
 EDGE = 3
 ROWS = 16
 SLOT = 32
-GROUP = 4
+GROUP = 16
+PAD = 4
 
 
 def sinc(values):
@@ -78,26 +79,24 @@
 
 def fill_base(vectors_t, base_ref, size, halo, side):
     n = vectors_t.shape[0]
+    stride = n + PAD
     for block in range(3):
         low, high, table = table_block(block, size, halo, side)
         out = jnp.dot(vectors_t[:, low:high], table, preferred_element_type=jnp.float32)
         for r in range(ROWS):
-            base_ref[pl.ds((block * ROWS + r) * n, n), :] = out[:, r * size : (r + 1) * size]
+            base_ref[pl.ds((block * ROWS + r) * stride, n), :] = out[:, r * size : (r + 1) * size]
 
 
 def build(base_ref, p, n, size):
+    stride = n + PAD
     blocks = []
     for block in range(3):
         halves = [
-            base_ref[pl.ds((block * ROWS + 8 * h) * n + p, 8, stride=n), :] for h in range(ROWS // 8)
+            base_ref[pl.ds((block * ROWS + 8 * h) * stride + p, 8, stride=stride), :] for h in range(ROWS // 8)
         ]
-        blocks.append(jnp.concatenate(halves, axis=0))
-    inner = [
-        pltpu.roll(blocks[1], ROWS * b, 1).astype(jnp.bfloat16) for b in range(size // ROWS - 2)
-    ]
-    return jnp.concatenate(
-        [blocks[0].astype(jnp.bfloat16)] + inner + [blocks[2].astype(jnp.bfloat16)], axis=0
-    )
+        blocks.append(jnp.concatenate(halves, axis=0).astype(jnp.bfloat16))
+    inner = [pltpu.roll(blocks[1], ROWS * b, 1) for b in range(size // ROWS - 2)]
+    return jnp.concatenate([blocks[0]] + inner + [blocks[2]], axis=0)
 
 
 def kernel(
@@ -119,6 +118,7 @@
     pad_ref,
     acc,
     cover,
+    held,
     sems,
 ):
     n, size, _ = pieces_h.shape
@@ -145,28 +145,42 @@
     for copy in copies:
         copy.wait()
 
-    def step(g, carry):
-        for k in range(GROUP):
-            p = g * GROUP + k
-            word = jnp.where(
-                lane < 64,
-                jnp.where(lane < 32, words_s[0, p], words_s[1, p]),
-                jnp.where(lane < 96, words_s[2, p], words_s[3, p]),
-            )
-            mask = (jnp.right_shift(word, bit) & 1).astype(jnp.float32)
-            mask = jnp.concatenate([mask, mask], axis=0).astype(jnp.bfloat16)
-            piece = pieces_v[p]
-            rows = [piece[16 * b : 16 * b + 16] * mask for b in range(size // 16)] + [mask]
-            right = build(right_base, p, n, size)
-            inner = jnp.dot(
-                jnp.concatenate(rows, axis=0), right, preferred_element_type=jnp.float32
-            )
-            cover[pl.ds(p, 1), :] = inner[size : size + 1]
+    def masked(p):
+        word = jnp.where(
+            lane < 64,
+            jnp.where(lane < 32, words_s[0, p], words_s[1, p]),
+            jnp.where(lane < 96, words_s[2, p], words_s[3, p]),
+        )
+        mask = (jnp.right_shift(word, bit) & 1).astype(jnp.float32)
+        mask = jnp.concatenate([mask, mask], axis=0).astype(jnp.bfloat16)
+        piece = pieces_v[p]
+        rows = [piece[16 * b : 16 * b + 16] * mask for b in range(size // 16)] + [mask, mask]
+        return jnp.concatenate(rows, axis=0)
+
+    def columns(g):
+        places = [g * GROUP + k for k in range(GROUP)]
+        dots = [
+            jnp.dot(masked(p), build(right_base, p, n, size), preferred_element_type=jnp.float32)
+            for p in places
+        ]
+        for k, p in enumerate(places):
+            cover[pl.ds(p, 1), :] = dots[k][size : size + 1]
             v = visit_s[0, p]
             factor = calib_s[0, v] * weights_s[0, v].astype(jnp.float32)
-            inner = (inner[:size] * factor).astype(jnp.bfloat16)
-            left = build(left_base, p, n, size)
-            acc[tile_s[0, p]] += jnp.dot(left, inner, preferred_element_type=jnp.float32)
+            held[k] = (dots[k][:size] * factor).astype(jnp.bfloat16)
+
+    def rows(g):
+        places = [g * GROUP + k for k in range(GROUP)]
+        dots = [
+            jnp.dot(build(left_base, p, n, size), held[k], preferred_element_type=jnp.float32)
+            for k, p in enumerate(places)
+        ]
+        for k, p in enumerate(places):
+            acc[tile_s[0, p]] += dots[k]
+
+    def step(g, carry):
+        columns(g)
+        rows(g)
         return carry
 
     lax.fori_loop(0, n // GROUP, step, 0)
@@ -204,11 +218,12 @@
         out_specs=vmem,
         scratch_shapes=[
             pltpu.VMEM((n, size, size), jnp.bfloat16),
-            pltpu.VMEM((3 * ROWS * n, size), jnp.float32),
-            pltpu.VMEM((3 * ROWS * n, size), jnp.float32),
+            pltpu.VMEM((3 * ROWS * (n + PAD), size), jnp.float32),
+            pltpu.VMEM((3 * ROWS * (n + PAD), size), jnp.float32),
             pltpu.VMEM((SLOT + 16, n), jnp.float32),
             pltpu.VMEM((tiles, size, size), jnp.float32),
             pltpu.VMEM((n, size), jnp.float32),
+            pltpu.VMEM((GROUP, size, size), jnp.bfloat16),
             pltpu.SemaphoreType.DMA((4,)),
         ],
         compiler_params=pltpu.CompilerParams(vmem_limit_bytes=56 * 1024 * 1024),

time: 68.1 us -> 32.7 us (0.48)
  Pallas kernels: 47 us -> 11.6 us
    pallas_call x1, Pallas kernels: 47 us -> 11.6 us  [partial_sums(): pl.pallas_call(functools.partial(kernel, tiles), out_shape=jax.ShapeDtype...]
where the time goes in v2:
time: 32.7 us; the launch traced here: 32.5 us
  Pallas kernels  11.6 us (35%)
  waiting for transfers between devices  10.9 us (33%)
  starting transfers between devices  7.3 us (22%)
  other arithmetic  1.34 us (4%)
  between operations  1.32 us (4%)
    pallas_call x1, Pallas kernels, partial_sums(): pl.pallas_call(functools.partial(kernel, tiles), out_shape=jax.ShapeDtype...  11.6 us
    all_to_all x1, waiting for transfers between devices, shards(): got = lax.all_to_all(sums, 'vis', split_axis=0, concat_axis=0, tiled=True)  9.65 us
    all_to_all x1, starting transfers between devices, shards(): got = lax.all_to_all(sums, 'vis', split_axis=0, concat_axis=0, tiled=True)  7.3 us
    ppermute x1, waiting for transfers between devices, shards(): lax.ppermute(scaled, 'band', [(b, (b + k) % bands) for b in range(bands)])  1.25 us
    mul x1, other arithmetic, shards(): scaled = band_gain[0] * coadd  0.65 us
  transfers between devices with their start and end apart: 2, of which 2 were waited for; matrix products, arithmetic and copies ran while one was open for 0% of the time, Pallas kernels for 0%

profile of v2, /device:TPU:0, one launch (start us, length us, event | category | flops | bytes accessed | tf_op | source)
XLA Modules:
  0.0 32.5 jit_solution(16494228504957224211)
XLA Ops:
  0.6 11.6 %partial_sums.1 = bf16[8,160,128]{2,1,0:T(8,128)(2,1)} custom-call(s32[1,192]{1,0:T(1,128)} %bitcast.20, s32[1,192]{1,0:T(1,128)} %visit_v.1, s32[4,192]{1,0:T(4,128)} %bitcast.19, f32[1,24]{1,0:T(1,128)} %calib_s.1, s32[1,24]{1,0:T(1,128)} %weights_s.1, s32[1,192]{1,0:T(1,128)} %bitcast.21, s32[1,192]{1,0:T(1,128)} %visit_v.1, f32[21,2,192]{2,1,0:T(2,128)} %bitcast.18, ...), custom_call_target="tpu_custom_call" | custom-call | tf_op jit(solution)/shard_map/partial_sums/pallas_call | solution.py:214
  12.2 7.3 %all-to-all-start = ((bf16[8,160,128]{2,1,0:T(8,128)(2,1)}), bf16[8,160,128]{2,1,0:T(8,128)(2,1)S(1)}, u32[]{:S(2)}, u32[]{:S(2)}) async-start(bf16[8,160,128]{2,1,0:T(8,128)(2,1)} %partial_sums.1), calls=%async_computation | async-start | bytes 655360 | tf_op jit(solution)/shard_map/all_to_all | solution.py:249
  20.2 9.6 %all-to-all-done = bf16[8,160,128]{2,1,0:T(8,128)(2,1)S(1)} async-done(((bf16[8,160,128]{2,1,0:T(8,128)(2,1)}), bf16[8,160,128]{2,1,0:T(8,128)(2,1)S(1)}, u32[]{:S(2)}, u32[]{:S(2)}) %all-to-all-start) | async-done | bytes 327712 | tf_op jit(solution)/shard_map/all_to_all | solution.py:249
  29.9 0.7 %broadcast_multiply_fusion = (f32[128,128]{1,0:T(8,128)S(1)}, f32[1,128,128]{2,1,0:T(8,128)}) fusion(f32[]{:T(128)} %bitcast.16, f32[13,128]{1,0:T(8,128)S(1)} %get-tuple-element.5, f32[102,128]{1,0:T(8,128)S(1)} %broadcast_in_dim.6, f32[13,128]{1,0:T(8,128)S(1)} %get-tuple-element.4, f32[160,128]{1,0:T(8,128)S(1)} %convert_reduce_fusion), kind=kLoop, calls=%fused_computation.3 | loop fusion | flops 81920 | bytes 262148 | tf_op jit(solution)/shard_map/mul | solution.py:261
  30.6 0.0 collective-permute-start
  30.6 1.3 %collective-permute-done = f32[128,128]{1,0:T(8,128)S(1)} collective-permute-done((f32[128,128]{1,0:T(8,128)S(1)}, f32[128,128]{1,0:T(8,128)S(1)}, u32[]{:S(2)}, u32[]{:S(2)}) %collective-permute-start) | collective-permute-done | bytes 65568 | tf_op jit(solution)/shard_map/ppermute | solution.py:265
  31.8 0.6 %add.3 = f32[128,128]{1,0:T(8,128)} add(f32[128,128]{1,0:T(8,128)S(1)} %get-tuple-element.2, f32[128,128]{1,0:T(8,128)S(1)} %collective-permute-done) | non-fusion elementwise | flops 16384 | bytes 196608 | tf_op jit(solution)/shard_map/add | solution.py:265
  (4 shorter events, 0.1 us)
Async XLA Ops:
  12.2 17.6 %all-to-all-start = ((bf16[8,160,128]{2,1,0:T(8,128)(2,1)}), bf16[8,160,128]{2,1,0:T(8,128)(2,1)S(1)}, u32[]{:S(2)}, u32[]{:S(2)}) async-start(bf16[8,160,128]{2,1,0:T(8,128)(2,1)} %partial_sums.1), calls=%async_computation | async-start | bytes 655360 | tf_op jit(solution)/shard_map/all_to_all | solution.py:249
  30.6 1.3 %collective-permute-start = (f32[128,128]{1,0:T(8,128)S(1)}, f32[128,128]{1,0:T(8,128)S(1)}, u32[]{:S(2)}, u32[]{:S(2)}) collective-permute-start(f32[128,128]{1,0:T(8,128)S(1)} %get-tuple-element.2), channel_id=1, source_target_pairs={{0,1},{1,0},{2,3},{3,2},{4,5},{5,4},{6,7},{7,6},{8,9},{9,8},{10,11... | collective-permute-start | bytes 196616 | tf_op jit(solution)/shard_map/ppermute | solution.py:265

commit v3 on v2

--- a/solution.py
+++ b/solution.py
@@ -11,7 +11,7 @@
 EDGE = 3
 ROWS = 16
 SLOT = 32
-GROUP = 16
+GROUP = 48
 PAD = 4
 
 
@@ -124,8 +124,8 @@
     n, size, _ = pieces_h.shape
     count = taps_v.shape[0]
     halo = (count - 1) // 2 + EDGE
-    chunks = sems.shape[0]
-    share = n // chunks
+    share = GROUP
+    chunks = n // share
     copies = [
         pltpu.make_async_copy(
             pieces_h.at[pl.ds(c * share, share)], pieces_v.at[pl.ds(c * share, share)], sems.at[c]
@@ -142,9 +142,6 @@
         fill_base(vec.astype(jnp.float32).T.astype(jnp.bfloat16), base_ref, size, halo, side)
     lane = lax.broadcasted_iota(jnp.int32, (8, size), 1)
     bit = lane & 31
-    for copy in copies:
-        copy.wait()
-
     def masked(p):
         word = jnp.where(
             lane < 64,
@@ -179,6 +176,8 @@
             acc[tile_s[0, p]] += dots[k]
 
     def step(g, carry):
+        spot = pl.ds(g * share, share)
+        pltpu.make_async_copy(pieces_h.at[spot], pieces_v.at[spot], sems.at[g]).wait()
         columns(g)
         rows(g)
         return carry
@@ -224,7 +223,7 @@
             pltpu.VMEM((tiles, size, size), jnp.float32),
             pltpu.VMEM((n, size), jnp.float32),
             pltpu.VMEM((GROUP, size, size), jnp.bfloat16),
-            pltpu.SemaphoreType.DMA((4,)),
+            pltpu.SemaphoreType.DMA((n // GROUP,)),
         ],
         compiler_params=pltpu.CompilerParams(vmem_limit_bytes=56 * 1024 * 1024),
         name="partial_sums",

time: 32.7 us -> 29.7 us (0.908)
  Pallas kernels: 11.6 us -> 8.58 us
    pallas_call x1, Pallas kernels: 11.6 us -> 8.58 us  [partial_sums(): pl.pallas_call(functools.partial(kernel, tiles), out_shape=jax.ShapeDtype...]
where the time goes in v3:
time: 29.7 us; the launch traced here: 29.4 us
  waiting for transfers between devices  10.9 us (37%)
  Pallas kernels  8.58 us (29%)
  starting transfers between devices  7.29 us (25%)
  other arithmetic  1.34 us (5%)
  between operations  1.32 us (4%)
    all_to_all x1, waiting for transfers between devices, shards(): got = lax.all_to_all(sums, 'vis', split_axis=0, concat_axis=0, tiled=True)  9.65 us
    pallas_call x1, Pallas kernels, partial_sums(): pl.pallas_call(functools.partial(kernel, tiles), out_shape=jax.ShapeDtype...  8.58 us
    all_to_all x1, starting transfers between devices, shards(): got = lax.all_to_all(sums, 'vis', split_axis=0, concat_axis=0, tiled=True)  7.29 us
    ppermute x1, waiting for transfers between devices, shards(): lax.ppermute(scaled, 'band', [(b, (b + k) % bands) for b in range(bands)])  1.25 us
    mul x1, other arithmetic, shards(): scaled = band_gain[0] * coadd  0.65 us
    add x1, other arithmetic, shards(): detection + lax.ppermute(scaled, 'band', [(b, (b + k) % bands) for b in r...  0.64 us
  transfers between devices with their start and end apart: 2, of which 2 were waited for; matrix products, arithmetic and copies ran while one was open for 0% of the time, Pallas kernels for 0%

profile of v3, /device:TPU:0, one launch (start us, length us, event | category | flops | bytes accessed | tf_op | source)
XLA Modules:
  0.0 29.4 jit_solution(15498166333953757800)
XLA Ops:
  0.6 8.6 %partial_sums.1 = bf16[8,160,128]{2,1,0:T(8,128)(2,1)} custom-call(s32[1,192]{1,0:T(1,128)} %bitcast.20, s32[1,192]{1,0:T(1,128)} %visit_v.1, s32[4,192]{1,0:T(4,128)} %bitcast.19, f32[1,24]{1,0:T(1,128)} %calib_s.1, s32[1,24]{1,0:T(1,128)} %weights_s.1, s32[1,192]{1,0:T(1,128)} %bitcast.21, s32[1,192]{1,0:T(1,128)} %visit_v.1, f32[21,2,192]{2,1,0:T(2,128)} %bitcast.18, ...), custom_call_target="tpu_custom_call" | custom-call | tf_op jit(solution)/shard_map/partial_sums/pallas_call | solution.py:213
  9.2 7.3 %all-to-all-start = ((bf16[8,160,128]{2,1,0:T(8,128)(2,1)}), bf16[8,160,128]{2,1,0:T(8,128)(2,1)S(1)}, u32[]{:S(2)}, u32[]{:S(2)}) async-start(bf16[8,160,128]{2,1,0:T(8,128)(2,1)} %partial_sums.1), calls=%async_computation | async-start | bytes 655360 | tf_op jit(solution)/shard_map/all_to_all | solution.py:248
  17.2 9.6 %all-to-all-done = bf16[8,160,128]{2,1,0:T(8,128)(2,1)S(1)} async-done(((bf16[8,160,128]{2,1,0:T(8,128)(2,1)}), bf16[8,160,128]{2,1,0:T(8,128)(2,1)S(1)}, u32[]{:S(2)}, u32[]{:S(2)}) %all-to-all-start) | async-done | bytes 327712 | tf_op jit(solution)/shard_map/all_to_all | solution.py:248
  26.9 0.7 %broadcast_multiply_fusion = (f32[128,128]{1,0:T(8,128)S(1)}, f32[1,128,128]{2,1,0:T(8,128)}) fusion(f32[]{:T(128)} %bitcast.16, f32[13,128]{1,0:T(8,128)S(1)} %get-tuple-element.5, f32[102,128]{1,0:T(8,128)S(1)} %broadcast_in_dim.6, f32[13,128]{1,0:T(8,128)S(1)} %get-tuple-element.4, f32[160,128]{1,0:T(8,128)S(1)} %convert_reduce_fusion), kind=kLoop, calls=%fused_computation.3 | loop fusion | flops 81920 | bytes 262148 | tf_op jit(solution)/shard_map/mul | solution.py:260
  27.6 0.0 collective-permute-start
  27.6 1.3 %collective-permute-done = f32[128,128]{1,0:T(8,128)S(1)} collective-permute-done((f32[128,128]{1,0:T(8,128)S(1)}, f32[128,128]{1,0:T(8,128)S(1)}, u32[]{:S(2)}, u32[]{:S(2)}) %collective-permute-start) | collective-permute-done | bytes 65568 | tf_op jit(solution)/shard_map/ppermute | solution.py:264
  28.8 0.6 %add.3 = f32[128,128]{1,0:T(8,128)} add(f32[128,128]{1,0:T(8,128)S(1)} %get-tuple-element.2, f32[128,128]{1,0:T(8,128)S(1)} %collective-permute-done) | non-fusion elementwise | flops 16384 | bytes 196608 | tf_op jit(solution)/shard_map/add | solution.py:264
  (4 shorter events, 0.1 us)
Async XLA Ops:
  9.2 17.6 %all-to-all-start = ((bf16[8,160,128]{2,1,0:T(8,128)(2,1)}), bf16[8,160,128]{2,1,0:T(8,128)(2,1)S(1)}, u32[]{:S(2)}, u32[]{:S(2)}) async-start(bf16[8,160,128]{2,1,0:T(8,128)(2,1)} %partial_sums.1), calls=%async_computation | async-start | bytes 655360 | tf_op jit(solution)/shard_map/all_to_all | solution.py:248
  27.6 1.3 %collective-permute-start = (f32[128,128]{1,0:T(8,128)S(1)}, f32[128,128]{1,0:T(8,128)S(1)}, u32[]{:S(2)}, u32[]{:S(2)}) collective-permute-start(f32[128,128]{1,0:T(8,128)S(1)} %get-tuple-element.2), channel_id=1, source_target_pairs={{0,1},{1,0},{2,3},{3,2},{4,5},{5,4},{6,7},{7,6},{8,9},{9,8},{10,11... | collective-permute-start | bytes 196616 | tf_op jit(solution)/shard_map/ppermute | solution.py:264

commit v4 on v3

--- a/solution.py
+++ b/solution.py
@@ -8,8 +8,10 @@
 from jax.experimental.pallas import tpu as pltpu
 from jax.sharding import PartitionSpec as P
 
+
 EDGE = 3
 ROWS = 16
+SQUARE = 4
 SLOT = 32
 GROUP = 48
 PAD = 4
@@ -27,7 +29,7 @@
 
 
 def tap_vectors(taps, shift, pad_ref):
-    count, n = taps.shape
+    count, _ = taps.shape
     kernel = (taps / jnp.sum(taps, axis=0, keepdims=True)).astype(jnp.bfloat16)
     steps = range(-EDGE, EDGE + 1)
     window = [lanczos(float(m) - shift) for m in steps]
@@ -100,7 +102,6 @@
 
 
 def kernel(
-    tiles,
     tile_s,
     visit_s,
     words_s,
@@ -111,7 +112,10 @@
     taps_v,
     shifts_v,
     pieces_h,
-    out_v,
+    own_v,
+    first_v,
+    second_v,
+    third_v,
     pieces_v,
     left_base,
     right_base,
@@ -121,6 +125,9 @@
     held,
     sems,
 ):
+    outs = (own_v, first_v, second_v, third_v)
+    rest = own_v.shape[0]
+    me = lax.axis_index("vis")
     n, size, _ = pieces_h.shape
     count = taps_v.shape[0]
     halo = (count - 1) // 2 + EDGE
@@ -142,6 +149,7 @@
         fill_base(vec.astype(jnp.float32).T.astype(jnp.bfloat16), base_ref, size, halo, side)
     lane = lax.broadcasted_iota(jnp.int32, (8, size), 1)
     bit = lane & 31
+
     def masked(p):
         word = jnp.where(
             lane < 64,
@@ -173,7 +181,8 @@
             for k, p in enumerate(places)
         ]
         for k, p in enumerate(places):
-            acc[tile_s[0, p]] += dots[k]
+            place = tile_s[0, p] ^ me
+            acc[(place & (SQUARE - 1)) * rest + lax.div(place, SQUARE)] += dots[k]
 
     def step(g, carry):
         spot = pl.ds(g * share, share)
@@ -195,15 +204,18 @@
     for v in range(weights_s.shape[1]):
         weight = jnp.where(visit_v[...] == v, weights_s[0, v].astype(jnp.float32), weight)
     row_weight = jnp.dot(table, vectors[0], preferred_element_type=jnp.float32) * weight
-    chosen_rows = [jnp.where(tile_v[...] == t, row_weight, 0.0) for t in range(tiles)]
-    den = jnp.dot(
-        jnp.concatenate(chosen_rows, axis=0).astype(jnp.bfloat16),
-        cover[...].astype(jnp.bfloat16),
-        preferred_element_type=jnp.float32,
-    )
-    for t in range(tiles):
-        out_v[t, :size, :] = acc[t].astype(out_v.dtype)
-        out_v[t, size:, :] = den[t * SLOT : (t + 1) * SLOT].astype(out_v.dtype)
+    for k, out_v in enumerate(outs):
+        chosen_rows = [
+            jnp.where(tile_v[...] == (SQUARE * j + k) ^ me, row_weight, 0.0) for j in range(rest)
+        ]
+        den = jnp.dot(
+            jnp.concatenate(chosen_rows, axis=0).astype(jnp.bfloat16),
+            cover[...].astype(jnp.bfloat16),
+            preferred_element_type=jnp.float32,
+        )
+        for j in range(rest):
+            out_v[j, :size, :] = acc[k * rest + j].astype(out_v.dtype)
+            out_v[j, size:, :] = den[j * SLOT : (j + 1) * SLOT].astype(out_v.dtype)
 
 
 def partial_sums(tiles, pieces, visit, tile, words, taps, shifts, calib, weights):
@@ -211,10 +223,13 @@
     smem = pl.BlockSpec(memory_space=pltpu.SMEM)
     vmem = pl.BlockSpec(memory_space=pltpu.VMEM)
     return pl.pallas_call(
-        functools.partial(kernel, tiles),
-        out_shape=jax.ShapeDtypeStruct((tiles, size + SLOT, size), jnp.bfloat16),
+        kernel,
+        out_shape=[
+            jax.ShapeDtypeStruct((tiles // SQUARE, size + SLOT, size), jnp.bfloat16 if k else jnp.float32)
+            for k in range(SQUARE)
+        ],
         in_specs=[smem] * 5 + [vmem] * 4 + [pl.BlockSpec(memory_space=pl.ANY)],
-        out_specs=vmem,
+        out_specs=[vmem] * SQUARE,
         scratch_shapes=[
             pltpu.VMEM((n, size, size), jnp.bfloat16),
             pltpu.VMEM((3 * ROWS * (n + PAD), size), jnp.float32),
@@ -225,9 +240,12 @@
             pltpu.VMEM((GROUP, size, size), jnp.bfloat16),
             pltpu.SemaphoreType.DMA((n // GROUP,)),
         ],
-        compiler_params=pltpu.CompilerParams(vmem_limit_bytes=56 * 1024 * 1024),
+        compiler_params=pltpu.CompilerParams(vmem_limit_bytes=28 * 1024 * 1024),
         name="partial_sums",
-    )(tile, visit, words, calib, weights, tile, visit, taps, shifts, pieces)
+    )(*(
+        pltpu.with_memory_space_constraint(x, pltpu.HBM)
+        for x in (tile, visit, words, calib, weights, tile, visit, taps, shifts, pieces)
+    ))
 
 
 def shards(pieces, visit, tile_map, good_columns, psf_taps, shifts, calib, weights, band_gain):
@@ -245,8 +263,18 @@
         calib,
         weights,
     )
-    got = lax.all_to_all(sums, "vis", split_axis=0, concat_axis=0, tiled=True)
-    total = jnp.sum(got.astype(jnp.float32), axis=0)
+    own, *others = sums
+    got = []
+    for k in range(SQUARE - 1, 0, -1):
+        got.append(lax.ppermute(others[k - 1], "vis", [(i, i ^ k) for i in range(tiles)]))
+    joint = [
+        own[j] + functools.reduce(jnp.add, [g[j].astype(jnp.float32) for g in got])
+        for j in range(tiles // SQUARE)
+    ]
+    total = joint[0]
+    for j in range(1, tiles // SQUARE):
+        ring = [(i, i ^ (SQUARE * j)) for i in range(tiles)]
+        total = total + lax.ppermute(joint[j].astype(jnp.bfloat16), "vis", ring).astype(jnp.float32)
     few = total[size:]
     den = jnp.concatenate(
         [

time: 29.7 us -> 25.3 us (0.85)
  waiting for transfers between devices: 10.9 us -> 7.18 us
  Pallas kernels: 8.58 us -> 7.89 us
    all_to_all x1 -> x0, waiting for transfers between devices: 9.65 us -> none  [shards(): got = lax.all_to_all(sums, 'vis', split_axis=0, concat_axis=0, tiled=True)]
    ppermute x0 -> x4, starting transfers between devices: none -> 7.32 us  [the longest x3 4.68 us: shards(): lax.ppermute(others[k - 1], 'vis', [(i, i ^ k) for i in range(tiles)])]
    all_to_all x1 -> x0, starting transfers between devices: 7.29 us -> none  [shards(): got = lax.all_to_all(sums, 'vis', split_axis=0, concat_axis=0, tiled=True)]
    ppermute x0 -> x4, waiting for transfers between devices: none -> 5.93 us  [the longest x3 4.26 us: shards(): lax.ppermute(others[k - 1], 'vis', [(i, i ^ k) for i in range(tiles)])]
    pallas_call x1, Pallas kernels: 8.58 us -> 7.89 us  [partial_sums(): pl.pallas_call(kernel, out_shape=[jax.ShapeDtypeStruct((tiles // SQUARE,...]
  transfers between devices with their start and end apart: 2 -> 5, of which waited for: 2 -> 5; matrix products, arithmetic and copies ran while one was open for 0% -> 0% of each run, Pallas kernels for 0% -> 0%
where the time goes in v4:
time: 25.3 us; the launch traced here: 25.1 us
  Pallas kernels  7.89 us (31%)
  starting transfers between devices  7.33 us (29%)
  waiting for transfers between devices  7.18 us (28%)
  other arithmetic  1.35 us (5%)
  between operations  1.33 us (5%)
    pallas_call x1, Pallas kernels, partial_sums(): pl.pallas_call(kernel, out_shape=[jax.ShapeDtypeStruct((tiles // SQUARE,...  7.89 us
    ppermute x3, starting transfers between devices, shards(): lax.ppermute(others[k - 1], 'vis', [(i, i ^ k) for i in range(tiles)])  4.68 us
    ppermute x3, waiting for transfers between devices, shards(): lax.ppermute(others[k - 1], 'vis', [(i, i ^ k) for i in range(tiles)])  4.26 us
    ppermute x1, starting transfers between devices, shards(): lax.ppermute(joint[j].astype(jnp.bfloat16), 'vis', ring).astype(jnp.float32)  2.64 us
    ppermute x1, waiting for transfers between devices, shards(): lax.ppermute(joint[j].astype(jnp.bfloat16), 'vis', ring).astype(jnp.float32)  1.67 us
    ppermute x1, waiting for transfers between devices, shards(): lax.ppermute(scaled, 'band', [(b, (b + k) % bands) for b in range(bands)])  1.25 us
    mul x1, other arithmetic, shards(): scaled = band_gain[0] * coadd  0.65 us
    add x1, other arithmetic, shards(): detection + lax.ppermute(scaled, 'band', [(b, (b + k) % bands) for b in r...  0.64 us
  transfers between devices with their start and end apart: 5, of which 5 were waited for; matrix products, arithmetic and copies ran while one was open for 0% of the time, Pallas kernels for 0%

profile of v4, /device:TPU:0, one launch (start us, length us, event | category | flops | bytes accessed | tf_op | source)
XLA Modules:
  0.0 25.1 jit_solution(16488199895328830326)
XLA Ops:
  0.6 7.9 %partial_sums.1 = (f32[2,160,128]{2,1,0:T(8,128)S(1)}, bf16[2,160,128]{2,1,0:T(8,128)(2,1)S(1)}, bf16[2,160,128]{2,1,0:T(8,128)(2,1)S(1)}, bf16[2,160,128]{2,1,0:T(8,128)(2,1)S(1)}) custom-call(s32[1,192]{1,0:T(1,128)} %bitcast.24, s32[1,192]{1,0:T(1,128)} %visit_v.1, s32[4,192]{1,0:T(4,128)} %bitcast.23, f32[1,24]{1,0:T(1,128)} %calib_s.1, ...), custom_call_target="tpu_custom_call" | custom-call | tf_op jit(solution)/shard_map/partial_sums/pallas_call | solution.py:225
  8.5 4.0 %collective-permute-start = (bf16[2,160,128]{2,1,0:T(8,128)(2,1)S(1)}, bf16[2,160,128]{2,1,0:T(8,128)(2,1)S(1)}, u32[]{:S(2)}, u32[]{:S(2)}) collective-permute-start(bf16[2,160,128]{2,1,0:T(8,128)(2,1)S(1)} %get-tuple-element.7), channel_id=1, source_target_pairs={{0,6},{2,4},{4,2},{6,0},{8,14},{10,12},{12,10},{14,8},{1,7},{3,5},... | collective-permute-start | bytes 245768 | tf_op jit(solution)/shard_map/ppermute | solution.py:269
  12.6 0.5 %collective-permute-start.1 = (bf16[2,160,128]{2,1,0:T(8,128)(2,1)S(1)}, bf16[2,160,128]{2,1,0:T(8,128)(2,1)S(1)}, u32[]{:S(2)}, u32[]{:S(2)}) collective-permute-start(bf16[2,160,128]{2,1,0:T(8,128)(2,1)S(1)} %get-tuple-element.8), channel_id=1, source_target_pairs={{0,4},{2,6},{4,0},{6,2},{8,12},{10,14},{12,8},{14,10},{1,5},{3,7},... | collective-permute-start | bytes 245768 | tf_op jit(solution)/shard_map/ppermute | solution.py:269
  13.0 0.2 collective-permute-start.2
  13.2 2.1 %collective-permute-done = bf16[2,160,128]{2,1,0:T(8,128)(2,1)S(1)} collective-permute-done((bf16[2,160,128]{2,1,0:T(8,128)(2,1)S(1)}, bf16[2,160,128]{2,1,0:T(8,128)(2,1)S(1)}, u32[]{:S(2)}, u32[]{:S(2)}) %collective-permute-start) | collective-permute-done | bytes 81952 | tf_op jit(solution)/shard_map/ppermute | solution.py:269
  15.3 1.9 %collective-permute-done.1 = bf16[2,160,128]{2,1,0:T(8,128)(2,1)S(1)} collective-permute-done((bf16[2,160,128]{2,1,0:T(8,128)(2,1)S(1)}, bf16[2,160,128]{2,1,0:T(8,128)(2,1)S(1)}, u32[]{:S(2)}, u32[]{:S(2)}) %collective-permute-start.1) | collective-permute-done | bytes 81952 | tf_op jit(solution)/shard_map/ppermute | solution.py:269
  17.2 0.3 %collective-permute-done.2 = bf16[2,160,128]{2,1,0:T(8,128)(2,1)S(1)} collective-permute-done((bf16[2,160,128]{2,1,0:T(8,128)(2,1)S(1)}, bf16[2,160,128]{2,1,0:T(8,128)(2,1)S(1)}, u32[]{:S(2)}, u32[]{:S(2)}) %collective-permute-start.2) | collective-permute-done | bytes 81952 | tf_op jit(solution)/shard_map/ppermute | solution.py:269
  17.5 2.6 %collective-permute-start.3 = (bf16[160,128]{1,0:T(8,128)(2,1)S(1)}, bf16[160,128]{1,0:T(8,128)(2,1)S(1)}, u32[]{:S(2)}, u32[]{:S(2)}) collective-permute-start(bf16[160,128]{1,0:T(8,128)(2,1)S(1)} %fusion), channel_id=1, source_target_pairs={{0,8},{2,10},{4,12},{6,14},{8,0},{10,2},{12,4},{14,6},{1,9},{3,11}... | collective-permute-start | bytes 122888 | tf_op jit(solution)/shard_map/ppermute | solution.py:277
  20.8 1.7 %collective-permute-done.3 = bf16[160,128]{1,0:T(8,128)(2,1)S(1)} collective-permute-done((bf16[160,128]{1,0:T(8,128)(2,1)S(1)}, bf16[160,128]{1,0:T(8,128)(2,1)S(1)}, u32[]{:S(2)}, u32[]{:S(2)}) %collective-permute-start.3) | collective-permute-done | bytes 40992 | tf_op jit(solution)/shard_map/ppermute | solution.py:277
  22.5 0.7 %broadcast_multiply_fusion = (f32[128,128]{1,0:T(8,128)S(1)}, f32[1,128,128]{2,1,0:T(8,128)}) fusion(f32[]{:T(128)} %bitcast.20, f32[13,128]{1,0:T(8,128)S(1)} %get-tuple-element.13, f32[102,128]{1,0:T(8,128)S(1)} %broadcast_in_dim.6, f32[13,128]{1,0:T(8,128)S(1)} %get-tuple-element.12, f32[160,128]{1,0:T(8,128)S(1)} %bitcast_add_fusion), kind=kLoop, calls=%fused_computation.5 | loop fusion | flops 81920 | bytes 262148 | tf_op jit(solution)/shard_map/mul | solution.py:288
  23.2 0.0 collective-permute-start.4
  23.2 1.3 %collective-permute-done.4 = f32[128,128]{1,0:T(8,128)S(1)} collective-permute-done((f32[128,128]{1,0:T(8,128)S(1)}, f32[128,128]{1,0:T(8,128)S(1)}, u32[]{:S(2)}, u32[]{:S(2)}) %collective-permute-start.4) | collective-permute-done | bytes 65568 | tf_op jit(solution)/shard_map/ppermute | solution.py:292
  24.5 0.6 %add.43 = f32[128,128]{1,0:T(8,128)} add(f32[128,128]{1,0:T(8,128)S(1)} %get-tuple-element.10, f32[128,128]{1,0:T(8,128)S(1)} %collective-permute-done.4) | non-fusion elementwise | flops 16384 | bytes 196608 | tf_op jit(solution)/shard_map/add | solution.py:292
  (5 shorter events, 0.1 us)
Async XLA Ops:
  8.5 6.8 %collective-permute-start = (bf16[2,160,128]{2,1,0:T(8,128)(2,1)S(1)}, bf16[2,160,128]{2,1,0:T(8,128)(2,1)S(1)}, u32[]{:S(2)}, u32[]{:S(2)}) collective-permute-start(bf16[2,160,128]{2,1,0:T(8,128)(2,1)S(1)} %get-tuple-element.7), channel_id=1, source_target_pairs={{0,6},{2,4},{4,2},{6,0},{8,14},{10,12},{12,10},{14,8},{1,7},{3,5},... | collective-permute-start | bytes 245768 | tf_op jit(solution)/shard_map/ppermute | solution.py:269
  12.6 4.6 %collective-permute-start.1 = (bf16[2,160,128]{2,1,0:T(8,128)(2,1)S(1)}, bf16[2,160,128]{2,1,0:T(8,128)(2,1)S(1)}, u32[]{:S(2)}, u32[]{:S(2)}) collective-permute-start(bf16[2,160,128]{2,1,0:T(8,128)(2,1)S(1)} %get-tuple-element.8), channel_id=1, source_target_pairs={{0,4},{2,6},{4,0},{6,2},{8,12},{10,14},{12,8},{14,10},{1,5},{3,7},... | collective-permute-start | bytes 245768 | tf_op jit(solution)/shard_map/ppermute | solution.py:269
  13.0 4.4 %collective-permute-start.2 = (bf16[2,160,128]{2,1,0:T(8,128)(2,1)S(1)}, bf16[2,160,128]{2,1,0:T(8,128)(2,1)S(1)}, u32[]{:S(2)}, u32[]{:S(2)}) collective-permute-start(bf16[2,160,128]{2,1,0:T(8,128)(2,1)S(1)} %get-tuple-element.9), channel_id=1, source_target_pairs={{0,2},{2,0},{4,6},{6,4},{8,10},{10,8},{12,14},{14,12},{1,3},{3,1},... | collective-permute-start | bytes 245768 | tf_op jit(solution)/shard_map/ppermute | solution.py:269
  17.5 5.0 %collective-permute-start.3 = (bf16[160,128]{1,0:T(8,128)(2,1)S(1)}, bf16[160,128]{1,0:T(8,128)(2,1)S(1)}, u32[]{:S(2)}, u32[]{:S(2)}) collective-permute-start(bf16[160,128]{1,0:T(8,128)(2,1)S(1)} %fusion), channel_id=1, source_target_pairs={{0,8},{2,10},{4,12},{6,14},{8,0},{10,2},{12,4},{14,6},{1,9},{3,11}... | collective-permute-start | bytes 122888 | tf_op jit(solution)/shard_map/ppermute | solution.py:277
  23.2 1.3 %collective-permute-start.4 = (f32[128,128]{1,0:T(8,128)S(1)}, f32[128,128]{1,0:T(8,128)S(1)}, u32[]{:S(2)}, u32[]{:S(2)}) collective-permute-start(f32[128,128]{1,0:T(8,128)S(1)} %get-tuple-element.10), channel_id=1, source_target_pairs={{0,1},{1,0},{2,3},{3,2},{4,5},{5,4},{6,7},{7,6},{8,9},{9,8},{10,11... | collective-permute-start | bytes 196616 | tf_op jit(solution)/shard_map/ppermute | solution.py:292

commit v5 on v4

--- a/solution.py
+++ b/solution.py
@@ -13,7 +13,7 @@
 ROWS = 16
 SQUARE = 4
 SLOT = 32
-GROUP = 48
+GROUP = 96
 PAD = 4
 
 
@@ -275,23 +275,27 @@
     for j in range(1, tiles // SQUARE):
         ring = [(i, i ^ (SQUARE * j)) for i in range(tiles)]
         total = total + lax.ppermute(joint[j].astype(jnp.bfloat16), "vis", ring).astype(jnp.float32)
-    few = total[size:]
-    den = jnp.concatenate(
-        [
-            few[:halo],
-            jnp.broadcast_to(few[halo], (size - 2 * halo, size)),
-            few[halo + 1 : 2 * halo + 1],
-        ],
-        axis=0,
-    )
-    coadd = total[:size] / jnp.maximum(den, 1.0)
-    scaled = band_gain[0] * coadd
+
+    def weighed(sums):
+        few = sums[size:]
+        den = jnp.concatenate(
+            [
+                few[:halo],
+                jnp.broadcast_to(few[halo], (size - 2 * halo, size)),
+                few[halo + 1 : 2 * halo + 1],
+            ],
+            axis=0,
+        )
+        return sums[:size] / jnp.maximum(den, 1.0)
+
+    scaled = band_gain[0] * weighed(total)
     detection = scaled
     bands = lax.axis_size("band")
     for k in range(1, bands):
         detection = detection + lax.ppermute(
             scaled, "band", [(b, (b + k) % bands) for b in range(bands)]
         )
+    coadd = weighed(lax.optimization_barrier(total))
     return (coadd[None], detection)
 
 

time: 25.3 us -> 24.3 us (0.960)
  waiting for transfers between devices: 7.18 us -> 6.49 us
  Pallas kernels: 7.89 us -> 7.4 us
    ppermute x1, waiting for transfers between devices: 1.25 us -> 0.57 us  [shards(): lax.ppermute(scaled, 'band', [(b, (b + k) % bands) for b in range(bands)])]
    broadcast_in_dim x0 -> x1, other arithmetic: none -> 0.65 us  [shards(): return (coadd[None], detection)]
    mul x1, other arithmetic: 0.65 us -> 0.03 us  [shards(): scaled = band_gain[0] * weighed(total)]
    pallas_call x1, Pallas kernels: 7.89 us -> 7.4 us  [partial_sums(): pl.pallas_call(kernel, out_shape=[jax.ShapeDtypeStruct((tiles // SQUARE,...]
  transfers between devices with their start and end apart: 5 -> 5, of which waited for: 5 -> 5; matrix products, arithmetic and copies ran while one was open for 0% -> 3% of each run, Pallas kernels for 0% -> 0%
where the time goes in v5:
time: 24.3 us; the launch traced here: 24.1 us
  starting transfers between devices  7.41 us (30%)
  Pallas kernels  7.4 us (30%)
  waiting for transfers between devices  6.49 us (27%)
  other arithmetic  1.37 us (6%)
  between operations  1.36 us (6%)
    pallas_call x1, Pallas kernels, partial_sums(): pl.pallas_call(kernel, out_shape=[jax.ShapeDtypeStruct((tiles // SQUARE,...  7.4 us
    ppermute x3, starting transfers between devices, shards(): lax.ppermute(others[k - 1], 'vis', [(i, i ^ k) for i in range(tiles)])  4.69 us
    ppermute x3, waiting for transfers between devices, shards(): lax.ppermute(others[k - 1], 'vis', [(i, i ^ k) for i in range(tiles)])  4.25 us
    ppermute x1, starting transfers between devices, shards(): lax.ppermute(joint[j].astype(jnp.bfloat16), 'vis', ring).astype(jnp.float32)  2.65 us
    ppermute x1, waiting for transfers between devices, shards(): lax.ppermute(joint[j].astype(jnp.bfloat16), 'vis', ring).astype(jnp.float32)  1.67 us
    broadcast_in_dim x1, other arithmetic, shards(): return (coadd[None], detection)  0.65 us
    add x1, other arithmetic, shards(): detection + lax.ppermute(scaled, 'band', [(b, (b + k) % bands) for b in r...  0.64 us
    ppermute x1, waiting for transfers between devices, shards(): lax.ppermute(scaled, 'band', [(b, (b + k) % bands) for b in range(bands)])  0.57 us
  transfers between devices with their start and end apart: 5, of which 5 were waited for; matrix products, arithmetic and copies ran while one was open for 3% of the time, Pallas kernels for 0%

profile of v5, /device:TPU:0, one launch (start us, length us, event | category | flops | bytes accessed | tf_op | source)
XLA Modules:
  0.0 24.1 jit_solution(6273704465133551656)
XLA Ops:
  0.6 7.4 %partial_sums.1 = (f32[2,160,128]{2,1,0:T(8,128)S(1)}, bf16[2,160,128]{2,1,0:T(8,128)(2,1)S(1)}, bf16[2,160,128]{2,1,0:T(8,128)(2,1)S(1)}, bf16[2,160,128]{2,1,0:T(8,128)(2,1)S(1)}) custom-call(s32[1,192]{1,0:T(1,128)} %bitcast.26, s32[1,192]{1,0:T(1,128)} %visit_v.1, s32[4,192]{1,0:T(4,128)} %bitcast.25, f32[1,24]{1,0:T(1,128)} %calib_s.1, ...), custom_call_target="tpu_custom_call" | custom-call | tf_op jit(solution)/shard_map/partial_sums/pallas_call | solution.py:225
  8.0 4.0 %collective-permute-start = (bf16[2,160,128]{2,1,0:T(8,128)(2,1)S(1)}, bf16[2,160,128]{2,1,0:T(8,128)(2,1)S(1)}, u32[]{:S(2)}, u32[]{:S(2)}) collective-permute-start(bf16[2,160,128]{2,1,0:T(8,128)(2,1)S(1)} %get-tuple-element.7), channel_id=1, source_target_pairs={{0,6},{2,4},{4,2},{6,0},{8,14},{10,12},{12,10},{14,8},{1,7},{3,5},... | collective-permute-start | bytes 245768 | tf_op jit(solution)/shard_map/ppermute | solution.py:269
  12.1 0.5 %collective-permute-start.1 = (bf16[2,160,128]{2,1,0:T(8,128)(2,1)S(1)}, bf16[2,160,128]{2,1,0:T(8,128)(2,1)S(1)}, u32[]{:S(2)}, u32[]{:S(2)}) collective-permute-start(bf16[2,160,128]{2,1,0:T(8,128)(2,1)S(1)} %get-tuple-element.8), channel_id=1, source_target_pairs={{0,4},{2,6},{4,0},{6,2},{8,12},{10,14},{12,8},{14,10},{1,5},{3,7},... | collective-permute-start | bytes 245768 | tf_op jit(solution)/shard_map/ppermute | solution.py:269
  12.5 0.2 collective-permute-start.2
  12.7 2.1 %collective-permute-done = bf16[2,160,128]{2,1,0:T(8,128)(2,1)S(1)} collective-permute-done((bf16[2,160,128]{2,1,0:T(8,128)(2,1)S(1)}, bf16[2,160,128]{2,1,0:T(8,128)(2,1)S(1)}, u32[]{:S(2)}, u32[]{:S(2)}) %collective-permute-start) | collective-permute-done | bytes 81952 | tf_op jit(solution)/shard_map/ppermute | solution.py:269
  14.9 1.9 %collective-permute-done.1 = bf16[2,160,128]{2,1,0:T(8,128)(2,1)S(1)} collective-permute-done((bf16[2,160,128]{2,1,0:T(8,128)(2,1)S(1)}, bf16[2,160,128]{2,1,0:T(8,128)(2,1)S(1)}, u32[]{:S(2)}, u32[]{:S(2)}) %collective-permute-start.1) | collective-permute-done | bytes 81952 | tf_op jit(solution)/shard_map/ppermute | solution.py:269
  16.7 0.3 %collective-permute-done.2 = bf16[2,160,128]{2,1,0:T(8,128)(2,1)S(1)} collective-permute-done((bf16[2,160,128]{2,1,0:T(8,128)(2,1)S(1)}, bf16[2,160,128]{2,1,0:T(8,128)(2,1)S(1)}, u32[]{:S(2)}, u32[]{:S(2)}) %collective-permute-start.2) | collective-permute-done | bytes 81952 | tf_op jit(solution)/shard_map/ppermute | solution.py:269
  17.0 2.6 %collective-permute-start.3 = (bf16[160,128]{1,0:T(8,128)(2,1)S(1)}, bf16[160,128]{1,0:T(8,128)(2,1)S(1)}, u32[]{:S(2)}, u32[]{:S(2)}) collective-permute-start(bf16[160,128]{1,0:T(8,128)(2,1)S(1)} %fusion.2), channel_id=1, source_target_pairs={{0,8},{2,10},{4,12},{6,14},{8,0},{10,2},{12,4},{14,6},{1,9},{3,11}... | collective-permute-start | bytes 122888 | tf_op jit(solution)/shard_map/ppermute | solution.py:277
  20.3 1.7 %collective-permute-done.3 = bf16[160,128]{1,0:T(8,128)(2,1)S(1)} collective-permute-done((bf16[160,128]{1,0:T(8,128)(2,1)S(1)}, bf16[160,128]{1,0:T(8,128)(2,1)S(1)}, u32[]{:S(2)}, u32[]{:S(2)}) %collective-permute-start.3) | collective-permute-done | bytes 40992 | tf_op jit(solution)/shard_map/ppermute | solution.py:277
  22.1 0.1 collective-permute-start.4
  22.2 0.7 %fusion.1 = f32[1,128,128]{2,1,0:T(8,128)} fusion(f32[160,128]{1,0:T(8,128)S(1)} %bitcast_add_fusion, f32[13,128]{1,0:T(8,128)S(1)} %get-tuple-element.13, f32[102,128]{1,0:T(8,128)S(1)} %broadcast_in_dim.9, f32[13,128]{1,0:T(8,128)S(1)} %get-tuple-element.12), kind=kLoop, calls=%fused_computation.5 | loop fusion | flops 65536 | bytes 196608 | tf_op jit(solution)/shard_map/broadcast_in_dim | solution.py:299
  22.9 0.6 %collective-permute-done.4 = f32[128,128]{1,0:T(8,128)S(1)} collective-permute-done((f32[128,128]{1,0:T(8,128)S(1)}, f32[128,128]{1,0:T(8,128)S(1)}, u32[]{:S(2)}, u32[]{:S(2)}) %collective-permute-start.4) | collective-permute-done | bytes 65568 | tf_op jit(solution)/shard_map/ppermute | solution.py:295
  23.4 0.6 %add.43 = f32[128,128]{1,0:T(8,128)} add(f32[128,128]{1,0:T(8,128)S(1)} %fusion, f32[128,128]{1,0:T(8,128)S(1)} %collective-permute-done.4) | non-fusion elementwise | flops 16384 | bytes 196608 | tf_op jit(solution)/shard_map/add | solution.py:295
  (9 shorter events, 0.1 us)
Async XLA Ops:
  8.0 6.8 %collective-permute-start = (bf16[2,160,128]{2,1,0:T(8,128)(2,1)S(1)}, bf16[2,160,128]{2,1,0:T(8,128)(2,1)S(1)}, u32[]{:S(2)}, u32[]{:S(2)}) collective-permute-start(bf16[2,160,128]{2,1,0:T(8,128)(2,1)S(1)} %get-tuple-element.7), channel_id=1, source_target_pairs={{0,6},{2,4},{4,2},{6,0},{8,14},{10,12},{12,10},{14,8},{1,7},{3,5},... | collective-permute-start | bytes 245768 | tf_op jit(solution)/shard_map/ppermute | solution.py:269
  12.1 4.6 %collective-permute-start.1 = (bf16[2,160,128]{2,1,0:T(8,128)(2,1)S(1)}, bf16[2,160,128]{2,1,0:T(8,128)(2,1)S(1)}, u32[]{:S(2)}, u32[]{:S(2)}) collective-permute-start(bf16[2,160,128]{2,1,0:T(8,128)(2,1)S(1)} %get-tuple-element.8), channel_id=1, source_target_pairs={{0,4},{2,6},{4,0},{6,2},{8,12},{10,14},{12,8},{14,10},{1,5},{3,7},... | collective-permute-start | bytes 245768 | tf_op jit(solution)/shard_map/ppermute | solution.py:269
  12.5 4.4 %collective-permute-start.2 = (bf16[2,160,128]{2,1,0:T(8,128)(2,1)S(1)}, bf16[2,160,128]{2,1,0:T(8,128)(2,1)S(1)}, u32[]{:S(2)}, u32[]{:S(2)}) collective-permute-start(bf16[2,160,128]{2,1,0:T(8,128)(2,1)S(1)} %get-tuple-element.9), channel_id=1, source_target_pairs={{0,2},{2,0},{4,6},{6,4},{8,10},{10,8},{12,14},{14,12},{1,3},{3,1},... | collective-permute-start | bytes 245768 | tf_op jit(solution)/shard_map/ppermute | solution.py:269
  17.0 5.0 %collective-permute-start.3 = (bf16[160,128]{1,0:T(8,128)(2,1)S(1)}, bf16[160,128]{1,0:T(8,128)(2,1)S(1)}, u32[]{:S(2)}, u32[]{:S(2)}) collective-permute-start(bf16[160,128]{1,0:T(8,128)(2,1)S(1)} %fusion.2), channel_id=1, source_target_pairs={{0,8},{2,10},{4,12},{6,14},{8,0},{10,2},{12,4},{14,6},{1,9},{3,11}... | collective-permute-start | bytes 122888 | tf_op jit(solution)/shard_map/ppermute | solution.py:277
  22.1 1.3 %collective-permute-start.4 = (f32[128,128]{1,0:T(8,128)S(1)}, f32[128,128]{1,0:T(8,128)S(1)}, u32[]{:S(2)}, u32[]{:S(2)}) collective-permute-start(f32[128,128]{1,0:T(8,128)S(1)} %fusion), channel_id=1, source_target_pairs={{0,1},{1,0},{2,3},{3,2},{4,5},{5,4},{6,7},{7,6},{8,9},{9,8},{10,11... | collective-permute-start | bytes 196616 | tf_op jit(solution)/shard_map/ppermute | solution.py:295

commit v6 on v5

--- a/solution.py
+++ b/solution.py
@@ -64,16 +64,22 @@
     start = {0: 0, 1: ROWS, 2: size - ROWS}[block]
     tap = lax.broadcasted_iota(jnp.int32, (depth, size), 0)
     lane = lax.broadcasted_iota(jnp.int32, (1, size), 1)
+    near = lax.broadcasted_iota(jnp.int32, (SLOT, size), 0)
+    far = lax.broadcasted_iota(jnp.int32, (SLOT, size), 1)
+    ahead = far - near if side == 0 else -far - near
     chunks = []
     for r in range(ROWS):
         row = start + r
-        if side == 0:
-            d = lane - row + halo
-            kind = min(row, EDGE) if row < size - EDGE else row - (size - EDGE) + EDGE + 1
-            slot = (kind - low) * SLOT + d
-        else:
-            d = row - lane + halo
-            slot = (kind_of(lane, size) - low) * SLOT + d
+        kind = min(row, EDGE) if row < size - EDGE else row - (size - EDGE) + EDGE + 1
+        if side == 0 or block == 1:
+            kind = kind if side == 0 else EDGE
+            taps = (ahead == (row - halo if side == 0 else -row - halo)).astype(jnp.float32)
+            parts = [jnp.zeros((rows, size), jnp.bfloat16) for rows in ((kind - low) * SLOT, (high - 1 - kind) * SLOT)]
+            parts.insert(1, taps.astype(jnp.bfloat16))
+            chunks.append(jnp.concatenate([x for x in parts if x.shape[0]], axis=0))
+            continue
+        d = row - lane + halo
+        slot = (kind_of(lane, size) - low) * SLOT + d
         slot = jnp.where((d >= 0) & (d <= 2 * halo), slot, -1)
         chunks.append((tap == slot).astype(jnp.float32).astype(jnp.bfloat16))
     return low * SLOT, high * SLOT, jnp.concatenate(chunks, axis=1)

time: 24.3 us -> 24.2 us (level)
  no operation moved by 1% of the time
where the time goes in v6:
time: 24.2 us; the launch traced here: 24.1 us
  starting transfers between devices  7.42 us (31%)
  Pallas kernels  7.4 us (31%)
  waiting for transfers between devices  6.48 us (27%)
  other arithmetic  1.37 us (6%)
  between operations  1.36 us (6%)
    pallas_call x1, Pallas kernels, partial_sums(): pl.pallas_call(kernel, out_shape=[jax.ShapeDtypeStruct((tiles // SQUARE,...  7.4 us
    ppermute x3, starting transfers between devices, shards(): lax.ppermute(others[k - 1], 'vis', [(i, i ^ k) for i in range(tiles)])  4.69 us
    ppermute x3, waiting for transfers between devices, shards(): lax.ppermute(others[k - 1], 'vis', [(i, i ^ k) for i in range(tiles)])  4.25 us
    ppermute x1, starting transfers between devices, shards(): lax.ppermute(joint[j].astype(jnp.bfloat16), 'vis', ring).astype(jnp.float32)  2.65 us
    ppermute x1, waiting for transfers between devices, shards(): lax.ppermute(joint[j].astype(jnp.bfloat16), 'vis', ring).astype(jnp.float32)  1.66 us
    broadcast_in_dim x1, other arithmetic, shards(): return (coadd[None], detection)  0.65 us
    add x1, other arithmetic, shards(): detection + lax.ppermute(scaled, 'band', [(b, (b + k) % bands) for b in r...  0.64 us
    ppermute x1, waiting for transfers between devices, shards(): lax.ppermute(scaled, 'band', [(b, (b + k) % bands) for b in range(bands)])  0.57 us
  transfers between devices with their start and end apart: 5, of which 5 were waited for; matrix products, arithmetic and copies ran while one was open for 3% of the time, Pallas kernels for 0%

profile of v6, /device:TPU:0, one launch (start us, length us, event | category | flops | bytes accessed | tf_op | source)
XLA Modules:
  0.0 24.1 jit_solution(14541082431533951510)
XLA Ops:
  0.6 7.4 %partial_sums.1 = (f32[2,160,128]{2,1,0:T(8,128)S(1)}, bf16[2,160,128]{2,1,0:T(8,128)(2,1)S(1)}, bf16[2,160,128]{2,1,0:T(8,128)(2,1)S(1)}, bf16[2,160,128]{2,1,0:T(8,128)(2,1)S(1)}) custom-call(s32[1,192]{1,0:T(1,128)} %bitcast.26, s32[1,192]{1,0:T(1,128)} %visit_v.1, s32[4,192]{1,0:T(4,128)} %bitcast.25, f32[1,24]{1,0:T(1,128)} %calib_s.1, ...), custom_call_target="tpu_custom_call" | custom-call | tf_op jit(solution)/shard_map/partial_sums/pallas_call | solution.py:231
  8.0 4.0 %collective-permute-start = (bf16[2,160,128]{2,1,0:T(8,128)(2,1)S(1)}, bf16[2,160,128]{2,1,0:T(8,128)(2,1)S(1)}, u32[]{:S(2)}, u32[]{:S(2)}) collective-permute-start(bf16[2,160,128]{2,1,0:T(8,128)(2,1)S(1)} %get-tuple-element.7), channel_id=1, source_target_pairs={{0,6},{2,4},{4,2},{6,0},{8,14},{10,12},{12,10},{14,8},{1,7},{3,5},... | collective-permute-start | bytes 245768 | tf_op jit(solution)/shard_map/ppermute | solution.py:275
  12.1 0.4 %collective-permute-start.1 = (bf16[2,160,128]{2,1,0:T(8,128)(2,1)S(1)}, bf16[2,160,128]{2,1,0:T(8,128)(2,1)S(1)}, u32[]{:S(2)}, u32[]{:S(2)}) collective-permute-start(bf16[2,160,128]{2,1,0:T(8,128)(2,1)S(1)} %get-tuple-element.8), channel_id=1, source_target_pairs={{0,4},{2,6},{4,0},{6,2},{8,12},{10,14},{12,8},{14,10},{1,5},{3,7},... | collective-permute-start | bytes 245768 | tf_op jit(solution)/shard_map/ppermute | solution.py:275
  12.5 0.2 collective-permute-start.2
  12.7 2.1 %collective-permute-done = bf16[2,160,128]{2,1,0:T(8,128)(2,1)S(1)} collective-permute-done((bf16[2,160,128]{2,1,0:T(8,128)(2,1)S(1)}, bf16[2,160,128]{2,1,0:T(8,128)(2,1)S(1)}, u32[]{:S(2)}, u32[]{:S(2)}) %collective-permute-start) | collective-permute-done | bytes 81952 | tf_op jit(solution)/shard_map/ppermute | solution.py:275
  14.9 1.9 %collective-permute-done.1 = bf16[2,160,128]{2,1,0:T(8,128)(2,1)S(1)} collective-permute-done((bf16[2,160,128]{2,1,0:T(8,128)(2,1)S(1)}, bf16[2,160,128]{2,1,0:T(8,128)(2,1)S(1)}, u32[]{:S(2)}, u32[]{:S(2)}) %collective-permute-start.1) | collective-permute-done | bytes 81952 | tf_op jit(solution)/shard_map/ppermute | solution.py:275
  16.7 0.3 %collective-permute-done.2 = bf16[2,160,128]{2,1,0:T(8,128)(2,1)S(1)} collective-permute-done((bf16[2,160,128]{2,1,0:T(8,128)(2,1)S(1)}, bf16[2,160,128]{2,1,0:T(8,128)(2,1)S(1)}, u32[]{:S(2)}, u32[]{:S(2)}) %collective-permute-start.2) | collective-permute-done | bytes 81952 | tf_op jit(solution)/shard_map/ppermute | solution.py:275
  17.0 2.7 %collective-permute-start.3 = (bf16[160,128]{1,0:T(8,128)(2,1)S(1)}, bf16[160,128]{1,0:T(8,128)(2,1)S(1)}, u32[]{:S(2)}, u32[]{:S(2)}) collective-permute-start(bf16[160,128]{1,0:T(8,128)(2,1)S(1)} %fusion.2), channel_id=1, source_target_pairs={{0,8},{2,10},{4,12},{6,14},{8,0},{10,2},{12,4},{14,6},{1,9},{3,11}... | collective-permute-start | bytes 122888 | tf_op jit(solution)/shard_map/ppermute | solution.py:283
  20.3 1.7 %collective-permute-done.3 = bf16[160,128]{1,0:T(8,128)(2,1)S(1)} collective-permute-done((bf16[160,128]{1,0:T(8,128)(2,1)S(1)}, bf16[160,128]{1,0:T(8,128)(2,1)S(1)}, u32[]{:S(2)}, u32[]{:S(2)}) %collective-permute-start.3) | collective-permute-done | bytes 40992 | tf_op jit(solution)/shard_map/ppermute | solution.py:283
  22.1 0.1 collective-permute-start.4
  22.2 0.7 %fusion.1 = f32[1,128,128]{2,1,0:T(8,128)} fusion(f32[160,128]{1,0:T(8,128)S(1)} %bitcast_add_fusion, f32[13,128]{1,0:T(8,128)S(1)} %get-tuple-element.13, f32[102,128]{1,0:T(8,128)S(1)} %broadcast_in_dim.9, f32[13,128]{1,0:T(8,128)S(1)} %get-tuple-element.12), kind=kLoop, calls=%fused_computation.5 | loop fusion | flops 65536 | bytes 196608 | tf_op jit(solution)/shard_map/broadcast_in_dim | solution.py:305
  22.8 0.6 %collective-permute-done.4 = f32[128,128]{1,0:T(8,128)S(1)} collective-permute-done((f32[128,128]{1,0:T(8,128)S(1)}, f32[128,128]{1,0:T(8,128)S(1)}, u32[]{:S(2)}, u32[]{:S(2)}) %collective-permute-start.4) | collective-permute-done | bytes 65568 | tf_op jit(solution)/shard_map/ppermute | solution.py:301
  23.4 0.6 %add.43 = f32[128,128]{1,0:T(8,128)} add(f32[128,128]{1,0:T(8,128)S(1)} %fusion, f32[128,128]{1,0:T(8,128)S(1)} %collective-permute-done.4) | non-fusion elementwise | flops 16384 | bytes 196608 | tf_op jit(solution)/shard_map/add | solution.py:301
  (9 shorter events, 0.1 us)
Async XLA Ops:
  8.0 6.8 %collective-permute-start = (bf16[2,160,128]{2,1,0:T(8,128)(2,1)S(1)}, bf16[2,160,128]{2,1,0:T(8,128)(2,1)S(1)}, u32[]{:S(2)}, u32[]{:S(2)}) collective-permute-start(bf16[2,160,128]{2,1,0:T(8,128)(2,1)S(1)} %get-tuple-element.7), channel_id=1, source_target_pairs={{0,6},{2,4},{4,2},{6,0},{8,14},{10,12},{12,10},{14,8},{1,7},{3,5},... | collective-permute-start | bytes 245768 | tf_op jit(solution)/shard_map/ppermute | solution.py:275
  12.1 4.6 %collective-permute-start.1 = (bf16[2,160,128]{2,1,0:T(8,128)(2,1)S(1)}, bf16[2,160,128]{2,1,0:T(8,128)(2,1)S(1)}, u32[]{:S(2)}, u32[]{:S(2)}) collective-permute-start(bf16[2,160,128]{2,1,0:T(8,128)(2,1)S(1)} %get-tuple-element.8), channel_id=1, source_target_pairs={{0,4},{2,6},{4,0},{6,2},{8,12},{10,14},{12,8},{14,10},{1,5},{3,7},... | collective-permute-start | bytes 245768 | tf_op jit(solution)/shard_map/ppermute | solution.py:275
  12.5 4.4 %collective-permute-start.2 = (bf16[2,160,128]{2,1,0:T(8,128)(2,1)S(1)}, bf16[2,160,128]{2,1,0:T(8,128)(2,1)S(1)}, u32[]{:S(2)}, u32[]{:S(2)}) collective-permute-start(bf16[2,160,128]{2,1,0:T(8,128)(2,1)S(1)} %get-tuple-element.9), channel_id=1, source_target_pairs={{0,2},{2,0},{4,6},{6,4},{8,10},{10,8},{12,14},{14,12},{1,3},{3,1},... | collective-permute-start | bytes 245768 | tf_op jit(solution)/shard_map/ppermute | solution.py:275
  17.0 5.0 %collective-permute-start.3 = (bf16[160,128]{1,0:T(8,128)(2,1)S(1)}, bf16[160,128]{1,0:T(8,128)(2,1)S(1)}, u32[]{:S(2)}, u32[]{:S(2)}) collective-permute-start(bf16[160,128]{1,0:T(8,128)(2,1)S(1)} %fusion.2), channel_id=1, source_target_pairs={{0,8},{2,10},{4,12},{6,14},{8,0},{10,2},{12,4},{14,6},{1,9},{3,11}... | collective-permute-start | bytes 122888 | tf_op jit(solution)/shard_map/ppermute | solution.py:283
  22.1 1.3 %collective-permute-start.4 = (f32[128,128]{1,0:T(8,128)S(1)}, f32[128,128]{1,0:T(8,128)S(1)}, u32[]{:S(2)}, u32[]{:S(2)}) collective-permute-start(f32[128,128]{1,0:T(8,128)S(1)} %fusion), channel_id=1, source_target_pairs={{0,1},{1,0},{2,3},{3,2},{4,5},{5,4},{6,7},{7,6},{8,9},{9,8},{10,11... | collective-permute-start | bytes 196616 | tf_op jit(solution)/shard_map/ppermute | solution.py:301
